TPU v7x, 512 devices: a whole 4x4x16 slice. The times are simulated.
512 devices in a mesh: ctx: 64 (over z_lo, y, core), grp: 8 (over x, z_hi).
Axes of the slice: x: 4, y: 4, z: 16 (z_hi: 2, z_lo: 8; z = z_hi * 8 + z_lo), core: 2. Of those that a mesh axis runs over, the one named last changes fastest.
Arguments:
- queries: bfloat16 [8192, 4096], P('ctx', 'grp'), may hold values from -6 to 6
- keys: bfloat16 [8192, 4096], P('ctx', 'grp'), may hold values from -6 to 6
- values: bfloat16 [8192, 4096], P('ctx', 'grp'), may hold values from -6 to 6
- block_order: int32 [128], replicated, may hold values from 0 to 127, each once
- token_ids: int32 [8192], P('ctx'), may hold values from 0 to 511
- stream_table: bfloat16 [4, 512, 8192], P(None, None, 'grp'), may hold values from -70 to 70
- short_filter: float32 [3, 7, 8192], P(None, None, 'grp'), may hold values from -2 to 2
- long_filter: bfloat16 [512, 128], P('grp'), may hold values from -0.5 to 0.5
- norm_gain: float32 [8192], P('grp'), may hold values from 0.1 to 1.9
Outputs:
- attended: bfloat16 [8192, 4096], P('ctx', 'grp')
- hyena_out: bfloat16 [8192, 8192], P('ctx', 'grp')
All inputs are finite; a program needn't handle non-finite values.
Results may differ from a plain program's by a relative error of at most 0.004.
Values may be sent and summed in bfloat16 or wider, within the bound.
No kernel may reach another device: no remote copies, remote signals or barrier semaphores. Data moves between devices by JAX's collectives and lax.ppermute only.
A program may use at most 128 MiB of HBM per device.

v0:
```python
import math

import jax
import jax.numpy as jnp
from jax import lax
from jax.sharding import PartitionSpec as P

HD = 128


neg_fill = -1e30
eps_norm = 1e-06


def passed_along(block, axis, distance):
    devices = range(lax.axis_size(axis))
    route = [(i - distance, i) for i in devices if i - distance in devices]
    return lax.ppermute(block, axis, route)


def block_positions(order, row_index, row_count):
    half_rows = row_count // 2
    slot = 2 * (row_index // row_count) + row_index % row_count // half_rows
    hits = slot[:, None] == jnp.arange(order.shape[0], dtype=jnp.int32)[None, :]
    block_start = jnp.sum(jnp.where(hits, order[None, :], 0), axis=1)
    return block_start * half_rows + row_index % half_rows


def attend_tile(running, keys_tile, values_tile, key_pos, query_heads, query_pos, score_scale):
    row_peak, row_total, weighted = running
    scores = (
        jnp.einsum("qhd,khd->hqk", query_heads, keys_tile, preferred_element_type=jnp.float32)
        * score_scale
    )
    visible = (key_pos[None, :] <= query_pos[:, None])[None]
    scores = jnp.where(visible, scores, neg_fill)
    new_peak = jnp.maximum(row_peak, jnp.max(scores, axis=2))
    weights = jnp.where(visible, jnp.exp(scores - new_peak[:, :, None]), 0.0)
    rescale = jnp.exp(row_peak - new_peak)
    row_total = row_total * rescale + jnp.sum(weights, axis=2)
    weighted = weighted * rescale.T[:, :, None] + jnp.einsum(
        "hqk,khd->qhd",
        weights.astype(jnp.bfloat16),
        values_tile,
        preferred_element_type=jnp.float32,
    )
    return (new_peak, row_total, weighted)


def guarded_tile(running, keys_tile, values_tile, key_pos, query_heads, query_pos, score_scale):
    return attend_tile(
        running, keys_tile, values_tile, key_pos, query_heads, query_pos, score_scale
    )


def lookup_rows(id_rows, stream_table):
    vocab_size = stream_table.shape[1]
    one_hot = (id_rows[:, None] == jnp.arange(vocab_size, dtype=jnp.int32)[None, :]).astype(
        jnp.bfloat16
    )
    return jnp.einsum("rv,svc->src", one_hot, stream_table, preferred_element_type=jnp.float32)


def short_mix(features, short_filter, out_rows):
    lead_rows = short_filter.shape[1] - 1
    results = []
    for stream in range(3):
        running = jnp.zeros((out_rows, features.shape[2]), jnp.float32)
        for lag_step in range(lead_rows + 1):
            running = (
                running
                + short_filter[stream, lag_step][None, :]
                * features[stream + 1, lead_rows - lag_step : lead_rows - lag_step + out_rows]
            )
        results.append(running)
    return results


def long_mix(extended, long_filter, out_rows):
    group_count, tap_count = long_filter.shape
    span_rows = extended.shape[0]
    lag_table = (
        jnp.arange(out_rows, dtype=jnp.int32)[:, None]
        + (tap_count - 1)
        - jnp.arange(span_rows, dtype=jnp.int32)[None, :]
    )
    inside = (lag_table >= 0) & (lag_table < tap_count)
    picked = long_filter[:, jnp.clip(lag_table, 0, tap_count - 1)]
    toeplitz = jnp.where(inside[None], picked, jnp.zeros((), long_filter.dtype))
    grouped = extended.reshape(span_rows, group_count, -1)
    result = jnp.einsum("gts,sgc->tgc", toeplitz, grouped, preferred_element_type=jnp.float32)
    return result.reshape(out_rows, -1)


def body(
    queries,
    keys,
    values,
    block_order,
    token_ids,
    stream_table,
    short_filter,
    long_filter,
    norm_gain,
):
    row_count = queries.shape[0]
    head_count = queries.shape[1] // HD
    device_index = lax.axis_index("ctx")
    query_pos = block_positions(
        block_order, device_index * row_count + jnp.arange(row_count, dtype=jnp.int32), row_count
    )
    query_heads = queries.reshape(row_count, head_count, HD)
    score_scale = 1.0 / math.sqrt(HD)
    initial = (
        jnp.full((head_count, row_count), neg_fill, jnp.float32),
        jnp.zeros((head_count, row_count), jnp.float32),
        jnp.zeros((row_count, head_count, HD), jnp.float32),
    )
    running = initial
    keys_piece = lax.all_gather(keys, "ctx", axis=0, tiled=True)
    values_piece = lax.all_gather(values, "ctx", axis=0, tiled=True)
    key_count = keys_piece.shape[0]
    key_pos_all = block_positions(block_order, jnp.arange(key_count, dtype=jnp.int32), row_count)
    keys_all = keys_piece.reshape(key_count, head_count, HD)
    values_all = values_piece.reshape(key_count, head_count, HD)
    tile_rows = 1024

    def one_tile(state, tile_index):
        first_key = tile_index * tile_rows
        keys_tile = lax.dynamic_slice_in_dim(keys_all, first_key, tile_rows, 0)
        values_tile = lax.dynamic_slice_in_dim(values_all, first_key, tile_rows, 0)
        key_pos = lax.dynamic_slice_in_dim(key_pos_all, first_key, tile_rows, 0)
        return (
            guarded_tile(
                state, keys_tile, values_tile, key_pos, query_heads, query_pos, score_scale
            ),
            None,
        )

    running, unused = lax.scan(
        one_tile, running, jnp.arange(key_count // tile_rows, dtype=jnp.int32)
    )
    row_peak, row_total, weighted = running
    attended = (
        (weighted / row_total.T[:, :, None])
        .astype(jnp.bfloat16)
        .reshape(row_count, head_count * HD)
    )
    token_count = token_ids.shape[0]
    lead_rows = short_filter.shape[1] - 1
    tap_count = long_filter.shape[1]
    first_row = device_index * token_count
    rim_ids = passed_along(token_ids[token_count - lead_rows :], "ctx", 1)
    id_rows = jnp.concatenate([rim_ids, token_ids])
    span_start = first_row - lead_rows
    features = lookup_rows(id_rows, stream_table)
    placed = span_start + jnp.arange(id_rows.shape[0], dtype=jnp.int32)
    features = features * (placed >= 0).astype(jnp.float32)[None, :, None]
    first_mix, second_mix, third_mix = short_mix(features, short_filter, token_count)
    product = (first_mix * third_mix).astype(jnp.bfloat16)
    product_rim = passed_along(product[token_count - (tap_count - 1) :], "ctx", 1)
    extended = jnp.concatenate([product_rim, product])
    residual = features[0, id_rows.shape[0] - token_count :]
    convolved = long_mix(extended, long_filter, token_count)
    mixed = residual + second_mix * convolved
    square_sum = lax.psum(jnp.sum(mixed * mixed, axis=1), "grp")
    channel_total = mixed.shape[1] * lax.axis_size("grp")
    inverse_rms = lax.rsqrt(square_sum / channel_total + eps_norm)
    hyena_out = (mixed * norm_gain[None, :] * inverse_rms[:, None]).astype(jnp.bfloat16)
    return (attended, hyena_out)


def solution(mesh):
    placed = (
        P("ctx", "grp"),
        P("ctx", "grp"),
        P("ctx", "grp"),
        P(),
        P("ctx"),
        P(None, None, "grp"),
        P(None, None, "grp"),
        P("grp", None),
        P("grp"),
    )
    return jax.shard_map(
        body,
        mesh=mesh,
        in_specs=placed,
        out_specs=(P("ctx", "grp"), P("ctx", "grp")),
        check_vma=False,
    )
```

profile of v0, /device:TPU:1, one launch (start us, length us, event | category | flops | bytes accessed | tf_op | source)
XLA Modules:
  0.0 333.8 jit_solution(7356627713634639187)
XLA Ops:
  10.4 4.6 %collective-permute-start = (s32[6]{0:T(128)S(1)}, s32[6]{0:T(128)S(1)}, u32[]{:S(2)}, u32[]{:S(2)}) collective-permute-start(s32[6]{0:T(128)S(1)} %slice.135), channel_id=1, source_target_pairs={{0,8},{8,16},{16,24},{24,32},{32,40},{40,48},{48,56},{56,64},{64,7... | collective-permute-start | bytes 80 | tf_op jit(solution)/shard_map/ppermute | solution.py:18
  19.8 3.0 multiply_bitcast_fusion
  23.8 1.9 collective-permute-start.1
  25.8 2.5 select_reduce_fusion
  28.5 66.0 %gather_fusion = bf16[32640,64]{1,0:T(8,128)(2,1)} fusion(bf16[64,128]{0,1:T(8,128)(2,1)S(1)} %copy.37, s32[32768]{0:T(1024)S(1)} %pad_clamp_fusion), kind=kCustom, calls=%fused_computation | custom fusion | bytes 8486400 | tf_op jit(solution)/shard_map/gather | solution.py:88
  94.4 8.6 %copy.38 = bf16[32640,64]{0,1:T(8,128)(2,1)} copy(bf16[32640,64]{1,0:T(8,128)(2,1)} %gather_fusion) | data formatting | bytes 8355840 | tf_op jit(solution)/shard_map/gather | solution.py:88
  103.1 15.9 %reshape.249 = bf16[128,255,64]{1,0,2:T(8,128)(2,1)} reshape(bf16[32640,64]{0,1:T(8,128)(2,1)} %copy.38) | data formatting | bytes 8355840 | tf_op jit(solution)/shard_map/gather | solution.py:88
  120.3 3.5 %fusion.20 = f32[64,16,128]{2,1,0:T(8,128)S(1)} fusion(bf16[255,64,16]{0,2,1:T(8,128)(2,1)} %bitcast.258, bf16[128,255,64]{1,0,2:T(8,128)(2,1)} %reshape.249, pred[128,255]{1,0:T(8,128)(4,1)S(1)} %fusion.73), kind=kOutput, calls=%fused_computation.28 | convolution fusion | flops 68935680 | bytes 5257088 | tf_op jit(solution)/shard_map/gts,sgc->tgc/dot_general | solution.py:91
  124.7 45.4 %psum.7 = f32[128]{0:T(128)S(1)} all-reduce(f32[128]{0:T(128)S(1)} %get-tuple-element.132), channel_id=1, replica_groups=mesh['ctx'=64,'grp'=8] {'grp'}, use_global_device_ids=true, to_apply=%region_7.8 | all-reduce | flops 128 | bytes 1024 | tf_op jit(solution)/shard_map/psum | solution.py:166
  171.0 12.1 %copy.32 = bf16[8192,512]{0,1:T(8,128)(2,1)} copy(bf16[8192,512]{1,0:T(8,128)(2,1)} %all-gather.5.cloned.1.call-done) | data formatting | bytes 16777216 | tf_op jit(solution)/shard_map/all_gather | solution.py:121
  183.0 95.5 %all-gather.3.cloned.1.call-done = bf16[8192,512]{0,1:T(8,128)(2,1)} async-done(((bf16[128,512]{0,1:T(8,128)(2,1)}), bf16[8192,512]{0,1:T(8,128)(2,1)}) %all-gather.3.cloned.1.call-update) | async-done | bytes 8388624 | tf_op jit(solution)/shard_map/all_gather | solution.py:120
  278.5 47.6 %while.15 = (s32[]{:T(128)}, f32[4,128]{1,0:T(4,128)S(1)}, f32[4,128]{1,0:T(4,128)S(1)}, f32[128,4,128]{0,2,1:T(8,128)S(1)}, s32[8]{0:T(128)S(1)}, /*index=5*/s3...) while((s32[]{:T(128)}, f32[4,128]{1,0:T(4,128)S(1)}, ...), condition=%wide.region_5.6_spmd.clone, body=%wide.region_2.5_spmd.clone.sunk | while | flops 275581952 | bytes 9614039 | solution.py:140
  280.0 1.9 fusion.112
  281.8 2.0 fusion.116
  285.9 1.9 fusion.112
  287.8 2.0 fusion.116
  291.9 1.9 fusion.112
  293.8 2.0 fusion.116
  297.8 1.9 fusion.112
  299.7 2.0 fusion.116
  305.7 2.0 fusion.116
  311.6 2.0 fusion.116
  317.6 2.0 fusion.116
  323.5 2.0 fusion.116
  (110 shorter events, 31.2 us)
Async XLA Ops:
  7.2 163.8 %all-gather.5.cloned.1.call-start = ((), (), s32[]{:S(2)}) async-start(), calls=%async_computation.1 | async-start | bytes 8519680 | tf_op jit(solution)/shard_map/all_gather | solution.py:121
  7.9 270.6 %all-gather.3.cloned.1.call-start = ((), (), s32[]{:S(2)}) async-start(), calls=%async_computation | async-start | bytes 8519680 | tf_op jit(solution)/shard_map/all_gather | solution.py:120
  10.4 8.8 %collective-permute-start = (s32[6]{0:T(128)S(1)}, s32[6]{0:T(128)S(1)}, u32[]{:S(2)}, u32[]{:S(2)}) collective-permute-start(s32[6]{0:T(128)S(1)} %slice.135), channel_id=1, source_target_pairs={{0,8},{8,16},{16,24},{24,32},{32,40},{40,48},{48,56},{56,64},{64,7... | collective-permute-start | bytes 80 | tf_op jit(solution)/shard_map/ppermute | solution.py:18
  22.8 2.9 copy-start.4
  22.9 5.5 %copy-start.2 = (bf16[64,128]{1,0:T(8,128)(2,1)S(1)}, bf16[64,128]{1,0:T(8,128)(2,1)}, u32[]{:S(2)}) copy-start(bf16[64,128]{1,0:T(8,128)(2,1)} %param.18) | copy-start | bytes 49156
  23.8 95.4 %collective-permute-start.1 = (bf16[127,1024]{1,0:T(8,128)(2,1)S(1)}, bf16[127,1024]{1,0:T(8,128)(2,1)S(1)}, u32[]{:S(2)}, u32[]{:S(2)}) collective-permute-start(bf16[127,1024]{1,0:T(8,128)(2,1)S(1)} %slice.204), channel_id=1, source_target_pairs={{0,8},{8,16},{16,24},{24,32},{32,40},{40,48},{48,56},{56,64},{64,7... | collective-permute-start | bytes 780296 | tf_op jit(solution)/shard_map/ppermute | solution.py:18
  103.1 15.9 %copy-start.1 = (bf16[128,512]{1,0:T(8,128)(2,1)S(1)}, bf16[128,512]{1,0:T(8,128)(2,1)}, u32[]{:S(2)}) copy-start(bf16[128,512]{1,0:T(8,128)(2,1)} %param.11) | copy-start | bytes 393220
  124.1 46.1 %copy-start.3 = (f32[1024]{0:T(1024)S(1)}, f32[1024]{0:T(1024)}, u32[]{:S(2)}) copy-start(f32[1024]{0:T(1024)} %param.19) | copy-start | bytes 12292
  171.0 107.5 %copy-start = (f32[128,4,128]{0,2,1:T(8,128)S(1)}, f32[128,4,128]{0,2,1:T(8,128)}, u32[]{:S(2)}) copy-start(f32[128,4,128]{0,2,1:T(8,128)} %custom-call.2) | copy-start | bytes 786436
Sparse Core Ops, SparseCore 0:
  10.1 132.7 all-gather.4
  145.5 132.9 all-gather.2
where the time goes:
time: 335 us; the launch traced here: 334 us
  local copies, waits for them, and re-layouts  115 us (34%)
  waiting for transfers between devices  96.5 us (29%)
  blocking collectives  45.4 us (14%)
  matrix products  37.6 us (11%)
  between operations  14.3 us (4%)
  other arithmetic  12.9 us (4%)
  starting transfers between devices  6.57 us (2%)
  loops' own time  5.68 us (2%)
    all_gather x1, waiting for transfers between devices, body(): keys_piece = lax.all_gather(keys, 'ctx', axis=0, tiled=True)  95.5 us
    gather x3, local copies, waits for them, and re-layouts, long_mix(): picked = long_filter[:, jnp.clip(lag_table, 0, tap_count - 1)]  90.5 us
    psum x1, blocking collectives, body(): square_sum = lax.psum(jnp.sum(mixed * mixed, axis=1), 'grp')  45.4 us
    dot_general x8, matrix products, attend_tile(): jnp.einsum('hqk,khd->qhd', weights.astype(jnp.bfloat16), values_tile, pre...  16.2 us
    dot_general x8, matrix products, attend_tile(): jnp.einsum('qhd,khd->hqk', query_heads, keys_tile, preferred_element_type...  14.8 us
    all_gather x1, local copies, waits for them, and re-layouts, body(): values_piece = lax.all_gather(values, 'ctx', axis=0, tiled=True)  12.1 us
  transfers between devices with their start and end apart: 4, of which 2 were waited for; matrix products, arithmetic and copies ran while one was open for 37% of the time, Pallas kernels for 0%

commit v1 on v0

v1 whole, which is shorter than its diff:
```python
import math

import jax
import jax.numpy as jnp
from jax import lax
from jax.experimental import pallas as pl
from jax.experimental.pallas import tpu as pltpu
from jax.sharding import Mesh, PartitionSpec as P

HD = 128
ROWS = 128
HALF = 64
QUADS = 4
YS = 4
SHORT = 7
TAPS = 128
GSIZE = 16
CHAN_BLOCK = 256
STAT_ROWS = 16

neg_fill = -1e30
eps_norm = 1e-06

f32 = jnp.float32
bf16 = jnp.bfloat16
CTX = ("zq", "zp", "y", "c")


def vmem_spec():
    return pl.BlockSpec(memory_space=pltpu.VMEM)


def smem_spec():
    return pl.BlockSpec(memory_space=pltpu.SMEM)


def params(**kw):
    return pltpu.CompilerParams(vmem_limit_bytes=48 * 1024 * 1024, **kw)


def pack_kernel(q_hbm, k_hbm, v_hbm, out_ref, buf, sems):
    copies = []
    for n, ref in enumerate((q_hbm, k_hbm, v_hbm)):
        copies.append(pltpu.make_async_copy(ref, buf.at[n], sems.at[n]))
        copies[-1].start()
    for n, copy in enumerate(copies):
        copy.wait()
        for head in range(QUADS):
            out_ref[head, n * ROWS : (n + 1) * ROWS] = buf[n, :, head * HD : (head + 1) * HD]


def pack(queries, keys, values):
    return pl.pallas_call(
        pack_kernel,
        out_shape=jax.ShapeDtypeStruct((QUADS, 3 * ROWS, HD), bf16),
        in_specs=[pl.BlockSpec(memory_space=pl.ANY)] * 3,
        out_specs=vmem_spec(),
        scratch_shapes=[
            pltpu.VMEM((3,) + queries.shape, bf16),
            pltpu.SemaphoreType.DMA((3,)),
        ],
        compiler_params=pltpu.CompilerParams(vmem_limit_bytes=60 * 1024 * 1024),
        cost_estimate=pl.CostEstimate(flops=0, bytes_accessed=786432, transcendentals=0),
        name="pack",
    )(queries, keys, values)


TILE = QUADS * ROWS


def attend_kernel(where_ref, order_ref, *refs):
    q_ref, kv_refs = refs[0], refs[1:5]
    out_ref, k_all, vt_all, scores, key_pos = refs[5:]
    zp, y, c = where_ref[0], where_ref[1], where_ref[2]
    scale2 = math.log2(math.e) / math.sqrt(HD)
    for n in range(4):
        low = ROWS if n == 0 else 0
        k_all[n] = kv_refs[n][:, low : low + ROWS].reshape(TILE, HD)
        vt_all[n] = kv_refs[n][:, low + ROWS : low + 2 * ROWS].reshape(TILE, HD).T
        kz = zp ^ (n & 1)
        kc = c ^ (n >> 1)
        for quad in range(QUADS):
            dev = quad * 16 + kz * 8 + y * 2 + kc
            for half in range(2):
                start = order_ref[2 * dev + half] * HALF
                key_pos[n, pl.ds((quad * 2 + half) * HALF, HALF), :] = (
                    lax.broadcasted_iota(jnp.int32, (HALF, 128), 0) + start
                )

    lane = lax.broadcasted_iota(jnp.int32, (1, 128), 1)

    def one_block(qy, carry):
        pieces = []
        for quad in range(QUADS):
            dev = quad * 16 + zp * 8 + qy * 2 + c
            first = order_ref[2 * dev] * HALF
            second = order_ref[2 * dev + 1] * HALF - HALF
            pieces.append(lane + jnp.where(lane < HALF, first, second))
        q_blk = q_ref[qy].reshape(TILE, HD)
        peak = jnp.full((1, TILE), neg_fill, f32)
        for n in range(4):
            s = lax.dot_general(
                k_all[n], q_blk, (((1,), (1,)), ((), ())), preferred_element_type=f32
            )
            kp = key_pos[n]
            cols = []
            for quad in range(QUADS):
                visible = kp <= pieces[quad]
                cols.append(jnp.where(visible, s[:, quad * 128 : (quad + 1) * 128], neg_fill))
            s = jnp.concatenate(cols, axis=1)
            scores[n] = s
            peak = jnp.maximum(peak, jnp.max(s, axis=0, keepdims=True))
        total = jnp.zeros((1, TILE), f32)
        acc = jnp.zeros((HD, TILE), f32)
        for n in range(4):
            p = jnp.exp2((scores[n] - peak) * scale2)
            total = total + jnp.sum(p, axis=0, keepdims=True)
            acc = acc + jnp.dot(vt_all[n], p.astype(bf16), preferred_element_type=f32)
        out_ref[qy, 0:HD, :] = acc.astype(bf16)
        rows = []
        for stat in (peak, total):
            rest = stat
            for piece in range(3):
                part = rest.astype(bf16).astype(f32)
                rows.append(part)
                rest = rest - part
        rows.append(jnp.zeros((STAT_ROWS - 6, TILE), f32))
        out_ref[qy, HD : HD + STAT_ROWS, :] = jnp.concatenate(rows, axis=0).astype(bf16)
        return carry

    lax.fori_loop(0, 4, one_block, 0)


def attend(where, order, q_all, kv_blocks):
    return pl.pallas_call(
        attend_kernel,
        out_shape=jax.ShapeDtypeStruct((YS, HD + STAT_ROWS, TILE), bf16),
        in_specs=[smem_spec(), smem_spec()] + [vmem_spec()] * 5,
        out_specs=vmem_spec(),
        scratch_shapes=[
            pltpu.VMEM((4, TILE, HD), bf16),
            pltpu.VMEM((4, HD, TILE), bf16),
            pltpu.VMEM((4, TILE, TILE), f32),
            pltpu.VMEM((4, TILE, 128), jnp.int32),
        ],
        compiler_params=params(),
        cost_estimate=pl.CostEstimate(
            flops=4 * 2048 * 2048 * 128, bytes_accessed=2 << 20, transcendentals=1 << 22
        ),
        name="attend",
    )(where, order, q_all, *kv_blocks)


def merge_kernel(part_ref, out_ref):
    scale2 = math.log2(math.e) / math.sqrt(HD)
    peaks, totals = [], []
    for n in range(YS):
        stats = part_ref[n, HD : HD + STAT_ROWS, :].astype(f32)
        peaks.append((stats[0:1] + stats[1:2]) + stats[2:3])
        totals.append((stats[3:4] + stats[4:5]) + stats[5:6])
    peak = jnp.maximum(jnp.maximum(peaks[0], peaks[1]), jnp.maximum(peaks[2], peaks[3]))
    factors = [jnp.exp2((one - peak) * scale2) for one in peaks]
    total = sum(f * t for f, t in zip(factors, totals))
    inverse = 1.0 / total
    acc = jnp.zeros((HD, TILE), f32)
    for n in range(YS):
        acc = acc + part_ref[n, 0:HD, :].astype(f32) * (factors[n] * inverse)
    for quad in range(QUADS):
        out_ref[quad] = acc[:, quad * ROWS : (quad + 1) * ROWS].T.astype(bf16)


def merge(parts):
    return pl.pallas_call(
        merge_kernel,
        out_shape=jax.ShapeDtypeStruct((QUADS, ROWS, HD), bf16),
        in_specs=[vmem_spec()],
        out_specs=vmem_spec(),
        compiler_params=params(),
        cost_estimate=pl.CostEstimate(flops=1 << 20, bytes_accessed=720896, transcendentals=4096),
        name="merge",
    )(parts)


def unpack_kernel(x_ref, out_ref):
    for head in range(QUADS):
        out_ref[:, head * HD : (head + 1) * HD] = x_ref[head]


def unpack(blocks):
    return pl.pallas_call(
        unpack_kernel,
        out_shape=jax.ShapeDtypeStruct((ROWS, QUADS * HD), bf16),
        in_specs=[vmem_spec()],
        out_specs=vmem_spec(),
        compiler_params=params(),
        cost_estimate=pl.CostEstimate(flops=0, bytes_accessed=262144, transcendentals=0),
        name="unpack",
    )(blocks)


EXT = 16 + 2 * ROWS


def hyena_kernel(
    rank_ref, far_ref, near_ref, own_ref, table_ref, short_ref, long_ref,
    mixed_ref, squares_ref, hot, feats_a, feats_b, prod, base, sq,
):
    step = pl.program_id(0)
    rank = rank_ref[0]
    vocab = table_ref.shape[1]

    @pl.when(step == 0)
    def _():
        lane = lax.broadcasted_iota(jnp.int32, (128, 128), 1)

        def column(ref, valid):
            ids = jnp.where(valid, ref[...], -1)
            return jnp.broadcast_to(ids, (128, 128)).T

        for ref, valid, low, at, count in (
            (far_ref, rank >= 2, 112, 0, 16),
            (near_ref, rank >= 1, 0, 16, 128),
            (own_ref, rank >= 0, 0, 144, 128),
        ):
            col = column(ref, valid)[low : low + count]
            for v in range(vocab // 128):
                hit = col == lane[low : low + count] + v * 128
                hot[at : at + count, v * 128 : (v + 1) * 128] = jnp.where(hit, 1.0, 0.0).astype(bf16)
        sq[...] = jnp.zeros_like(sq)
        tap = lax.broadcasted_iota(jnp.int32, (TAPS, 2 * ROWS), 0)
        spot = lax.broadcasted_iota(jnp.int32, (TAPS, 2 * ROWS), 1)
        flip = jnp.where(tap + spot == TAPS, 1.0, 0.0).astype(bf16)
        base[...] = jnp.dot(long_ref[...], flip, preferred_element_type=f32)

    feats_a[...] = jnp.dot(hot[...], table_ref[1], preferred_element_type=f32)
    feats_b[...] = jnp.dot(hot[...], table_ref[3], preferred_element_type=f32)

    def short_mix(ref, stream, low, count, lanes):
        running = jnp.zeros((count, 128), f32)
        for k in range(SHORT):
            running = running + short_ref[stream, k : k + 1, lanes] * ref[low - k : low - k + count, lanes]
        return running

    for lb in range(CHAN_BLOCK // 128):
        lanes = slice(lb * 128, (lb + 1) * 128)
        for low in (16, 144):
            one = short_mix(feats_a, 0, low, 128, lanes)
            three = short_mix(feats_b, 2, low, 128, lanes)
            prod[low - 16 : low + 112, lanes] = (one * three).astype(bf16)
    feats_a[128:, :] = jnp.dot(hot[128:, :], table_ref[2], preferred_element_type=f32)
    feats_b[144:, :] = jnp.dot(hot[144:, :], table_ref[0], preferred_element_type=f32)
    chan = lax.broadcasted_iota(jnp.int32, (ROWS, CHAN_BLOCK), 1) // GSIZE
    groups_here = CHAN_BLOCK // GSIZE
    window = base[pl.ds(pl.multiple_of(step * groups_here, groups_here), groups_here)]
    conv = jnp.zeros((ROWS, CHAN_BLOCK), f32)
    for g in range(groups_here):
        row = jnp.broadcast_to(window[g : g + 1], (ROWS, 2 * ROWS))
        lags = pltpu.roll(row, 0, 1, stride=1, stride_axis=0).astype(bf16)
        every = jnp.dot(lags, prod[...], preferred_element_type=f32)
        conv = jnp.where(chan == g, every, conv)
    for lb in range(CHAN_BLOCK // 128):
        lanes = slice(lb * 128, (lb + 1) * 128)
        acc = conv[:, lanes]
        two = short_mix(feats_a, 1, 144, ROWS, lanes)
        mixed = feats_b[144:, lanes] + two * acc
        mixed_ref[:, lanes] = mixed
        sq[...] += mixed * mixed

    @pl.when(step == pl.num_programs(0) - 1)
    def _():
        squares_ref[...] = jnp.sum(sq[...].T, axis=0, keepdims=True)


def hyena(rank, far, near, own, table, short_filter, long_filter):
    streams, vocab, channels = table.shape
    return pl.pallas_call(
        hyena_kernel,
        grid=(channels // CHAN_BLOCK,),
        out_shape=(
            jax.ShapeDtypeStruct((ROWS, channels), f32),
            jax.ShapeDtypeStruct((1, ROWS), f32),
        ),
        in_specs=[
            smem_spec(),
            pl.BlockSpec((1, ROWS), lambda i: (0, 0)),
            pl.BlockSpec((1, ROWS), lambda i: (0, 0)),
            pl.BlockSpec((1, ROWS), lambda i: (0, 0)),
            pl.BlockSpec((streams, vocab, CHAN_BLOCK), lambda i: (0, 0, i)),
            pl.BlockSpec((3, SHORT, CHAN_BLOCK), lambda i: (0, 0, i)),
            pl.BlockSpec(long_filter.shape, lambda i: (0, 0)),
        ],
        out_specs=(
            pl.BlockSpec((ROWS, CHAN_BLOCK), lambda i: (0, i)),
            pl.BlockSpec((1, ROWS), lambda i: (0, 0)),
        ),
        scratch_shapes=[
            pltpu.VMEM((EXT, vocab), bf16),
            pltpu.VMEM((EXT, CHAN_BLOCK), f32),
            pltpu.VMEM((EXT, CHAN_BLOCK), f32),
            pltpu.VMEM((2 * ROWS, CHAN_BLOCK), bf16),
            pltpu.VMEM((long_filter.shape[0], 2 * ROWS), f32),
            pltpu.VMEM((ROWS, 128), f32),
        ],
        compiler_params=pltpu.CompilerParams(
            vmem_limit_bytes=60 * 1024 * 1024, dimension_semantics=("arbitrary",)
        ),
        cost_estimate=pl.CostEstimate(flops=1 << 30, bytes_accessed=5 << 20, transcendentals=0),
        name="hyena",
    )(rank, far, near, own, table, short_filter, long_filter)


def norm_kernel(channels, mixed_ref, squares_ref, gain_ref, out_ref):
    mean = squares_ref[...] / channels
    inverse = jnp.broadcast_to(lax.rsqrt(mean + eps_norm), (ROWS, ROWS)).T
    for lb in range(mixed_ref.shape[1] // 128):
        lanes = slice(lb * 128, (lb + 1) * 128)
        out_ref[:, lanes] = (mixed_ref[:, lanes] * gain_ref[:, lanes] * inverse).astype(bf16)


def norm(mixed, squares, gain, channels):
    def kernel(*refs):
        norm_kernel(channels, *refs)

    return pl.pallas_call(
        kernel,
        out_shape=jax.ShapeDtypeStruct(mixed.shape, bf16),
        in_specs=[vmem_spec()] * 3,
        out_specs=vmem_spec(),
        compiler_params=params(),
        cost_estimate=pl.CostEstimate(flops=1 << 18, bytes_accessed=800000, transcendentals=128),
        name="norm",
    )(mixed, squares, gain)


def across(squares, stride):
    groups = lax.axis_size("g")
    if stride >= groups:
        return squares
    return squares + lax.ppermute(squares, "g", [(i ^ stride, i) for i in range(groups)])


def body(
    queries, keys, values, block_order, token_ids, stream_table, short_filter, long_filter, norm_gain
):
    groups = lax.axis_size("g")
    zp, y, c = lax.axis_index("zp"), lax.axis_index("y"), lax.axis_index("c")
    rank = ((lax.axis_index("zq") * 2 + zp) * 4 + y) * 2 + c
    devices = QUADS * 2 * YS * 2

    own = lax.all_to_all(pack(queries, keys, values), "zq", 0, 0)

    near = lax.ppermute(token_ids, CTX, [(i, i + 1) for i in range(devices - 1)])
    far = lax.ppermute(token_ids, CTX, [(i, i + 2) for i in range(devices - 2)])
    mixed, squares = hyena(
        rank.reshape(1), far[None], near[None], token_ids[None],
        stream_table, short_filter, long_filter,
    )
    squares = across(squares, 1)
    own, mixed, squares = lax.optimization_barrier((own, mixed, squares))

    q_all = lax.all_to_all(jnp.broadcast_to(own[None, :, 0:ROWS], (YS, QUADS, ROWS, HD)), "y", 0, 0)
    swap = [(0, 1), (1, 0)]
    kv_own = own[:, ROWS:]
    kv_z = lax.ppermute(kv_own, "zp", swap)
    kv_c = lax.ppermute(kv_own, "c", swap)
    kv_zc = lax.ppermute(kv_z, "c", swap)
    where = jnp.stack([zp, y, c])
    parts = attend(where, block_order, q_all, [own, kv_z, kv_c, kv_zc])
    parts, squares = lax.optimization_barrier((parts, squares))
    parts = lax.all_to_all(parts, "y", 0, 0)
    for stride in (2, 4):
        squares = across(squares, stride)
    parts, squares = lax.optimization_barrier((parts, squares))
    blocks = lax.all_to_all(merge(parts), "zq", 0, 0)
    hyena_out = norm(mixed, squares, norm_gain[None], stream_table.shape[2] * groups)
    blocks, hyena_out = lax.optimization_barrier((blocks, hyena_out))
    return (unpack(blocks), hyena_out)


def solution(mesh):
    groups = mesh.shape["grp"]
    fine = Mesh(mesh.devices.reshape(QUADS, 2, YS, 2, groups), CTX + ("g",))
    placed = (
        P(CTX, "g"),
        P(CTX, "g"),
        P(CTX, "g"),
        P(),
        P(CTX),
        P(None, None, "g"),
        P(None, None, "g"),
        P("g", None),
        P("g"),
    )
    return jax.shard_map(
        body,
        mesh=fine,
        in_specs=placed,
        out_specs=(P(CTX, "g"), P(CTX, "g")),
        check_vma=False,
    )
```

time: 335 us -> 117 us (0.35)
  the two profiles are of different devices: /device:TPU:1 before, /device:TPU:14 now
where the time goes in v1:
time: 117 us; the launch traced here: 116 us
  starting transfers between devices  65.9 us (56%)
  waiting for transfers between devices  26.1 us (22%)
  Pallas kernels  20.9 us (18%)
  local copies, waits for them, and re-layouts  1.52 us (1%)
    ppermute x3, starting transfers between devices, across(): lax.ppermute(squares, 'g', [(i ^ stride, i) for i in range(groups)])  15.1 us
    all_to_all x1, starting transfers between devices, body(): blocks = lax.all_to_all(merge(parts), 'zq', 0, 0)  12.5 us
    ppermute x3, waiting for transfers between devices, across(): lax.ppermute(squares, 'g', [(i ^ stride, i) for i in range(groups)])  11.5 us
    all_to_all x1, starting transfers between devices, body(): own = lax.all_to_all(pack(queries, keys, values), 'zq', 0, 0)  11.2 us
    pallas_call x1, Pallas kernels, attend(): pl.pallas_call(attend_kernel, out_shape=jax.ShapeDtypeStruct((YS, HD + ST...  9.11 us
    all_to_all x1, waiting for transfers between devices, body(): blocks = lax.all_to_all(merge(parts), 'zq', 0, 0)  9.08 us
    all_to_all x1, starting transfers between devices, body(): lax.all_to_all(jnp.broadcast_to(own[None, :, 0:ROWS], (YS, QUADS, ROWS, H...  8.68 us
    pallas_call x1, Pallas kernels, hyena(): pl.pallas_call(hyena_kernel, grid=(channels // CHAN_BLOCK,), out_shape=(j...  7.56 us
  transfers between devices with their start and end apart: 12, of which 7 were waited for; matrix products, arithmetic and copies ran while one was open for 1% of the time, Pallas kernels for 7%

profile of v1, /device:TPU:14, one launch (start us, length us, event | category | flops | bytes accessed | tf_op | source)
XLA Modules:
  0.0 116.0 jit_solution(18275306450478622066)
XLA Ops:
  0.6 1.8 %pack.1 = bf16[4,384,128]{2,1,0:T(8,128)(2,1)} custom-call(bf16[128,512]{1,0:T(8,128)(2,1)} %q_hbm.1, bf16[128,512]{1,0:T(8,128)(2,1)} %k_hbm.1, bf16[128,512]{1,0:T(8,128)(2,1)} %v_hbm.1), custom_call_target="tpu_custom_call" | custom-call | bytes 786432 | tf_op jit(solution)/shard_map/pack/pallas_call | solution.py:53
  2.5 11.2 %all-to-all-start = ((bf16[4,384,128]{2,1,0:T(8,128)(2,1)}), bf16[4,384,128]{2,1,0:T(8,128)(2,1)S(1)}, u32[]{:S(2)}, u32[]{:S(2)}) async-start(bf16[4,384,128]{2,1,0:T(8,128)(2,1)} %pack.1), calls=%async_computation | async-start | bytes 786432 | tf_op jit(solution)/shard_map/all_to_all | solution.py:350
  13.7 3.5 %collective-permute-start = (s32[128]{0:T(128)}, s32[128]{0:T(128)S(1)}, u32[]{:S(2)}, u32[]{:S(2)}) collective-permute-start(s32[128]{0:T(128)} %param.13), channel_id=1, source_target_pairs={{0,16},{8,24},{16,32},{24,40},{32,48},{40,56},{48,64},{56,72},{64,... | collective-permute-start | bytes 1544 | tf_op jit(solution)/shard_map/ppermute | solution.py:353
  17.1 1.9 %collective-permute-start.1 = (s32[128]{0:T(128)}, s32[128]{0:T(128)S(1)}, u32[]{:S(2)}, u32[]{:S(2)}) collective-permute-start(s32[128]{0:T(128)} %param.13), channel_id=1, source_target_pairs={{0,8},{8,16},{16,24},{24,32},{32,40},{40,48},{48,56},{56,64},{64,7... | collective-permute-start | bytes 1544 | tf_op jit(solution)/shard_map/ppermute | solution.py:352
  19.2 2.9 %collective-permute-done.1 = s32[128]{0:T(128)S(1)} collective-permute-done((s32[128]{0:T(128)}, s32[128]{0:T(128)S(1)}, u32[]{:S(2)}, u32[]{:S(2)}) %collective-permute-start.1) | collective-permute-done | bytes 544 | tf_op jit(solution)/shard_map/ppermute | solution.py:352
  22.7 7.6 %hyena.1 = (f32[128,1024]{1,0:T(8,128)}, f32[1,128]{1,0:T(1,128)}) custom-call(s32[1]{0:T(128)} %bitcast.3.rank_ref, s32[1,128]{1,0:T(1,128)} %bitcast.10, s32[1,128]{1,0:T(1,128)} %bitcast.11, s32[1,128]{1,0:T(1,128)} %bitcast.9, bf16[4,512,1024]{2,1,0:T(8,128)(2,1)} %table_ref.1, f32[3,7,1024]{2,1,0:T(8,128)} %short_ref.1, bf16[64,128]{1,0:T(8,128)(2,1)} %long_ref.1), custom_call_target="tpu_custom_call" | custom-call | flops 1073741824 | bytes 5242880 | tf_op jit(solution)/shard_map/hyena/pallas_call | solution.py:276
  30.3 9.1 %collective-permute-start.2 = (f32[1,128]{1,0:T(1,128)}, f32[1,128]{1,0:T(1,128)S(1)}, u32[]{:S(2)}, u32[]{:S(2)}) collective-permute-start(f32[1,128]{1,0:T(1,128)} %get-tuple-element.14), channel_id=1, source_target_pairs={{1,0},{0,1},{3,2},{2,3},{5,4},{4,5},{7,6},{6,7},{9,8},{8,9},{11,10... | collective-permute-start | bytes 1544 | tf_op jit(solution)/shard_map/ppermute | solution.py:339
  39.4 5.1 %collective-permute-done.2 = f32[1,128]{1,0:T(1,128)S(1)} collective-permute-done((f32[1,128]{1,0:T(1,128)}, f32[1,128]{1,0:T(1,128)S(1)}, u32[]{:S(2)}, u32[]{:S(2)}) %collective-permute-start.2) | collective-permute-done | bytes 544 | tf_op jit(solution)/shard_map/ppermute | solution.py:339
  45.2 3.8 %collective-permute-start.3 = (bf16[4,256,128]{2,1,0:T(8,128)(2,1)S(1)}, bf16[4,256,128]{2,1,0:T(8,128)(2,1)S(1)}, u32[]{:S(2)}, u32[]{:S(2)}) collective-permute-start(bf16[4,256,128]{2,1,0:T(8,128)(2,1)S(1)} %slice.7), channel_id=1, source_target_pairs={{0,64},{64,0},{1,65},{65,1},{2,66},{66,2},{3,67},{67,3},{4,68},{68... | collective-permute-start | bytes 786440 | tf_op jit(solution)/shard_map/ppermute | solution.py:364
  49.1 0.9 broadcast_in_dim.21
  50.0 8.7 %all-to-all-start.1 = ((bf16[4,4,128,128]{3,2,1,0:T(8,128)(2,1)}), bf16[4,4,128,128]{3,2,1,0:T(8,128)(2,1)S(1)}, u32[]{:S(2)}, u32[]{:S(2)}) async-start(bf16[4,4,128,128]{3,2,1,0:T(8,128)(2,1)} %broadcast_in_dim.21), calls=%async_computation.1 | async-start | bytes 1048576 | tf_op jit(solution)/shard_map/all_to_all | solution.py:361
  58.7 1.9 %collective-permute-start.4 = (bf16[4,256,128]{2,1,0:T(8,128)(2,1)S(1)}, bf16[4,256,128]{2,1,0:T(8,128)(2,1)S(1)}, u32[]{:S(2)}, u32[]{:S(2)}) collective-permute-start(bf16[4,256,128]{2,1,0:T(8,128)(2,1)S(1)} %slice.7), channel_id=1, source_target_pairs={{0,8},{8,0},{1,9},{9,1},{2,10},{10,2},{3,11},{11,3},{4,12},{12,4},... | collective-permute-start | bytes 786440 | tf_op jit(solution)/shard_map/ppermute | solution.py:365
  60.6 2.4 %collective-permute-start.5 = (bf16[4,256,128]{2,1,0:T(8,128)(2,1)S(1)}, bf16[4,256,128]{2,1,0:T(8,128)(2,1)S(1)}, u32[]{:S(2)}, u32[]{:S(2)}) collective-permute-start(bf16[4,256,128]{2,1,0:T(8,128)(2,1)S(1)} %collective-permute-done.3.refs_2_), channel_id=1, source_target_pairs={{0,8},{8,0},{1,9},{9,1},{2,10},{10,2},{3,11},{11,3},{4,12},{12,4},... | collective-permute-start | bytes 786440 | tf_op jit(solution)/shard_map/ppermute | solution.py:366
  63.1 2.5 %all-to-all-done.1.refs_0_ = bf16[4,4,128,128]{3,2,1,0:T(8,128)(2,1)S(1)} async-done(((bf16[4,4,128,128]{3,2,1,0:T(8,128)(2,1)}), bf16[4,4,128,128]{3,2,1,0:T(8,128)(2,1)S(1)}, u32[]{:S(2)}, u32[]{:S(2)}) %all-to-all-start.1) | async-done | bytes 524320 | tf_op jit(solution)/shard_map/all_to_all | solution.py:361
  65.6 9.1 %attend.1 = bf16[4,144,512]{2,1,0:T(8,128)(2,1)} custom-call(s32[3]{0:T(128)S(1)} %pad_add_fusion.where_ref, s32[128]{0:T(128)S(1)} %copy-done.2, bf16[4,4,128,128]{3,2,1,0:T(8,128)(2,1)S(1)} %all-to-all-done.1.refs_0_, bf16[4,384,128]{2,1,0:T(8,128)(2,1)S(1)} %all-to-all-done.refs_1_, bf16[4,256,128]{2,1,0:T(8,128)(2,1)S(1)} %collective-permute-done.3.refs_2_, ...), custom_call_target="tpu_custom_call" | custom-call | flops 2147483648 | bytes 2097152 | tf_op jit(solution)/shard_map/attend/pallas_call | solution.py:135
  74.7 4.9 %all-to-all-start.2 = ((bf16[4,144,512]{2,1,0:T(8,128)(2,1)}), bf16[4,144,512]{2,1,0:T(8,128)(2,1)S(1)}, u32[]{:S(2)}, u32[]{:S(2)}) async-start(bf16[4,144,512]{2,1,0:T(8,128)(2,1)} %attend.1), calls=%async_computation.2 | async-start | bytes 1179648 | tf_op jit(solution)/shard_map/all_to_all | solution.py:370
  79.6 2.7 %collective-permute-start.6 = (f32[1,128]{1,0:T(1,128)S(1)}, f32[1,128]{1,0:T(1,128)S(1)}, u32[]{:S(2)}, u32[]{:S(2)}) collective-permute-start(f32[1,128]{1,0:T(1,128)S(1)} %add.21), channel_id=1, source_target_pairs={{2,0},{3,1},{0,2},{1,3},{6,4},{7,5},{4,6},{5,7},{10,8},{11,9},{8,1... | collective-permute-start | bytes 1544 | tf_op jit(solution)/shard_map/ppermute | solution.py:339
  82.3 2.7 %collective-permute-done.6 = f32[1,128]{1,0:T(1,128)S(1)} collective-permute-done((f32[1,128]{1,0:T(1,128)S(1)}, f32[1,128]{1,0:T(1,128)S(1)}, u32[]{:S(2)}, u32[]{:S(2)}) %collective-permute-start.6) | collective-permute-done | bytes 544 | tf_op jit(solution)/shard_map/ppermute | solution.py:339
  85.1 3.3 %collective-permute-start.7 = (f32[1,128]{1,0:T(1,128)S(1)}, f32[1,128]{1,0:T(1,128)S(1)}, u32[]{:S(2)}, u32[]{:S(2)}) collective-permute-start(f32[1,128]{1,0:T(1,128)S(1)} %add.22), channel_id=1, source_target_pairs={{4,0},{5,1},{6,2},{7,3},{0,4},{1,5},{2,6},{3,7},{12,8},{13,9},{14,... | collective-permute-start | bytes 1544 | tf_op jit(solution)/shard_map/ppermute | solution.py:339
  88.4 3.6 %collective-permute-done.7 = f32[1,128]{1,0:T(1,128)S(1)} collective-permute-done((f32[1,128]{1,0:T(1,128)S(1)}, f32[1,128]{1,0:T(1,128)S(1)}, u32[]{:S(2)}, u32[]{:S(2)}) %collective-permute-start.7) | collective-permute-done | bytes 544 | tf_op jit(solution)/shard_map/ppermute | solution.py:339
  92.0 0.9 merge.1
  92.9 12.5 %all-to-all-start.3 = ((bf16[4,128,128]{2,1,0:T(8,128)(2,1)}), bf16[4,128,128]{2,1,0:T(8,128)(2,1)S(1)}, u32[]{:S(2)}, u32[]{:S(2)}) async-start(bf16[4,128,128]{2,1,0:T(8,128)(2,1)} %merge.1), calls=%async_computation.3 | async-start | bytes 262144 | tf_op jit(solution)/shard_map/all_to_all | solution.py:374
  105.4 0.8 norm.1
  106.2 9.1 %all-to-all-done.3.x_ref = bf16[4,128,128]{2,1,0:T(8,128)(2,1)S(1)} async-done(((bf16[4,128,128]{2,1,0:T(8,128)(2,1)}), bf16[4,128,128]{2,1,0:T(8,128)(2,1)S(1)}, u32[]{:S(2)}, u32[]{:S(2)}) %all-to-all-start.3) | async-done | bytes 131104 | tf_op jit(solution)/shard_map/all_to_all | solution.py:374
  (23 shorter events, 2.2 us)
Async XLA Ops:
  0.6 65.0 %copy-start.2 = (s32[128]{0:T(128)S(1)}, s32[128]{0:T(128)}, u32[]{:S(2)}) copy-start(s32[128]{0:T(128)} %order_ref.1) | copy-start | bytes 1540
  2.5 42.7 %all-to-all-start = ((bf16[4,384,128]{2,1,0:T(8,128)(2,1)}), bf16[4,384,128]{2,1,0:T(8,128)(2,1)S(1)}, u32[]{:S(2)}, u32[]{:S(2)}) async-start(bf16[4,384,128]{2,1,0:T(8,128)(2,1)} %pack.1), calls=%async_computation | async-start | bytes 786432 | tf_op jit(solution)/shard_map/all_to_all | solution.py:350
  13.7 5.6 %collective-permute-start = (s32[128]{0:T(128)}, s32[128]{0:T(128)S(1)}, u32[]{:S(2)}, u32[]{:S(2)}) collective-permute-start(s32[128]{0:T(128)} %param.13), channel_id=1, source_target_pairs={{0,16},{8,24},{16,32},{24,40},{32,48},{40,56},{48,64},{56,72},{64,... | collective-permute-start | bytes 1544 | tf_op jit(solution)/shard_map/ppermute | solution.py:353
  17.1 5.0 %collective-permute-start.1 = (s32[128]{0:T(128)}, s32[128]{0:T(128)S(1)}, u32[]{:S(2)}, u32[]{:S(2)}) collective-permute-start(s32[128]{0:T(128)} %param.13), channel_id=1, source_target_pairs={{0,8},{8,16},{16,24},{24,32},{32,40},{40,48},{48,56},{56,64},{64,7... | collective-permute-start | bytes 1544 | tf_op jit(solution)/shard_map/ppermute | solution.py:352
  19.2 2.9 %copy-start.3 = (s32[128]{0:T(128)}, s32[128]{0:T(128)S(1)}, u32[]{:S(2)}) copy-start(s32[128]{0:T(128)S(1)} %collective-permute-done) | copy-start | bytes 1540
  22.2 0.6 copy-start.4
  30.3 14.2 %collective-permute-start.2 = (f32[1,128]{1,0:T(1,128)}, f32[1,128]{1,0:T(1,128)S(1)}, u32[]{:S(2)}, u32[]{:S(2)}) collective-permute-start(f32[1,128]{1,0:T(1,128)} %get-tuple-element.14), channel_id=1, source_target_pairs={{1,0},{0,1},{3,2},{2,3},{5,4},{4,5},{7,6},{6,7},{9,8},{8,9},{11,10... | collective-permute-start | bytes 1544 | tf_op jit(solution)/shard_map/ppermute | solution.py:339
  45.2 15.4 %collective-permute-start.3 = (bf16[4,256,128]{2,1,0:T(8,128)(2,1)S(1)}, bf16[4,256,128]{2,1,0:T(8,128)(2,1)S(1)}, u32[]{:S(2)}, u32[]{:S(2)}) collective-permute-start(bf16[4,256,128]{2,1,0:T(8,128)(2,1)S(1)} %slice.7), channel_id=1, source_target_pairs={{0,64},{64,0},{1,65},{65,1},{2,66},{66,2},{3,67},{67,3},{4,68},{68... | collective-permute-start | bytes 786440 | tf_op jit(solution)/shard_map/ppermute | solution.py:364
  50.0 15.6 %all-to-all-start.1 = ((bf16[4,4,128,128]{3,2,1,0:T(8,128)(2,1)}), bf16[4,4,128,128]{3,2,1,0:T(8,128)(2,1)S(1)}, u32[]{:S(2)}, u32[]{:S(2)}) async-start(bf16[4,4,128,128]{3,2,1,0:T(8,128)(2,1)} %broadcast_in_dim.21), calls=%async_computation.1 | async-start | bytes 1048576 | tf_op jit(solution)/shard_map/all_to_all | solution.py:361
  58.7 4.4 %collective-permute-start.4 = (bf16[4,256,128]{2,1,0:T(8,128)(2,1)S(1)}, bf16[4,256,128]{2,1,0:T(8,128)(2,1)S(1)}, u32[]{:S(2)}, u32[]{:S(2)}) collective-permute-start(bf16[4,256,128]{2,1,0:T(8,128)(2,1)S(1)} %slice.7), channel_id=1, source_target_pairs={{0,8},{8,0},{1,9},{9,1},{2,10},{10,2},{3,11},{11,3},{4,12},{12,4},... | collective-permute-start | bytes 786440 | tf_op jit(solution)/shard_map/ppermute | solution.py:365
  60.6 5.0 %collective-permute-start.5 = (bf16[4,256,128]{2,1,0:T(8,128)(2,1)S(1)}, bf16[4,256,128]{2,1,0:T(8,128)(2,1)S(1)}, u32[]{:S(2)}, u32[]{:S(2)}) collective-permute-start(bf16[4,256,128]{2,1,0:T(8,128)(2,1)S(1)} %collective-permute-done.3.refs_2_), channel_id=1, source_target_pairs={{0,8},{8,0},{1,9},{9,1},{2,10},{10,2},{3,11},{11,3},{4,12},{12,4},... | collective-permute-start | bytes 786440 | tf_op jit(solution)/shard_map/ppermute | solution.py:366
  63.1 42.3 %copy-start = (f32[128,1024]{1,0:T(8,128)S(1)}, f32[128,1024]{1,0:T(8,128)}, u32[]{:S(2)}) copy-start(f32[128,1024]{1,0:T(8,128)} %get-tuple-element.20.refs_0_) | copy-start | bytes 1572868
  63.1 42.3 %copy-start.1 = (f32[1024]{0:T(1024)S(1)}, f32[1024]{0:T(1024)}, u32[]{:S(2)}) copy-start(f32[1024]{0:T(1024)} %param.17) | copy-start | bytes 12292
  74.7 17.3 %all-to-all-start.2 = ((bf16[4,144,512]{2,1,0:T(8,128)(2,1)}), bf16[4,144,512]{2,1,0:T(8,128)(2,1)S(1)}, u32[]{:S(2)}, u32[]{:S(2)}) async-start(bf16[4,144,512]{2,1,0:T(8,128)(2,1)} %attend.1), calls=%async_computation.2 | async-start | bytes 1179648 | tf_op jit(solution)/shard_map/all_to_all | solution.py:370
  79.6 5.5 %collective-permute-start.6 = (f32[1,128]{1,0:T(1,128)S(1)}, f32[1,128]{1,0:T(1,128)S(1)}, u32[]{:S(2)}, u32[]{:S(2)}) collective-permute-start(f32[1,128]{1,0:T(1,128)S(1)} %add.21), channel_id=1, source_target_pairs={{2,0},{3,1},{0,2},{1,3},{6,4},{7,5},{4,6},{5,7},{10,8},{11,9},{8,1... | collective-permute-start | bytes 1544 | tf_op jit(solution)/shard_map/ppermute | solution.py:339
  85.1 7.0 %collective-permute-start.7 = (f32[1,128]{1,0:T(1,128)S(1)}, f32[1,128]{1,0:T(1,128)S(1)}, u32[]{:S(2)}, u32[]{:S(2)}) collective-permute-start(f32[1,128]{1,0:T(1,128)S(1)} %add.22), channel_id=1, source_target_pairs={{4,0},{5,1},{6,2},{7,3},{0,4},{1,5},{2,6},{3,7},{12,8},{13,9},{14,... | collective-permute-start | bytes 1544 | tf_op jit(solution)/shard_map/ppermute | solution.py:339
  92.9 22.4 %all-to-all-start.3 = ((bf16[4,128,128]{2,1,0:T(8,128)(2,1)}), bf16[4,128,128]{2,1,0:T(8,128)(2,1)S(1)}, u32[]{:S(2)}, u32[]{:S(2)}) async-start(bf16[4,128,128]{2,1,0:T(8,128)(2,1)} %merge.1), calls=%async_computation.3 | async-start | bytes 262144 | tf_op jit(solution)/shard_map/all_to_all | solution.py:374

commit v2 on v1

--- a/solution.py
+++ b/solution.py
@@ -6,6 +6,7 @@
 from jax.experimental import pallas as pl
 from jax.experimental.pallas import tpu as pltpu
 from jax.sharding import Mesh, PartitionSpec as P
+
 
 HD = 128
 ROWS = 128
@@ -23,7 +24,7 @@
 
 f32 = jnp.float32
 bf16 = jnp.bfloat16
-CTX = ("zq", "zp", "y", "c")
+CTX = ("zp", "zq", "y", "c")
 
 
 def vmem_spec():
@@ -68,87 +69,116 @@
 TILE = QUADS * ROWS
 
 
-def attend_kernel(where_ref, order_ref, *refs):
-    q_ref, kv_refs = refs[0], refs[1:5]
-    out_ref, k_all, vt_all, scores, key_pos = refs[5:]
+ACC = HD + STAT_ROWS
+
+
+def attend_kernel(members, resume, final, where_ref, order_ref, q_ref, *refs):
+    count = len(members)
+    kv_refs, refs = refs[:count], refs[count:]
+    if resume:
+        acc_in, peak_in, *refs = refs
+    if final:
+        out_ref, k_all, vt_all, scores = refs
+    else:
+        acc_out, peak_out, k_all, vt_all, scores = refs
     zp, y, c = where_ref[0], where_ref[1], where_ref[2]
     scale2 = math.log2(math.e) / math.sqrt(HD)
-    for n in range(4):
-        low = ROWS if n == 0 else 0
-        k_all[n] = kv_refs[n][:, low : low + ROWS].reshape(TILE, HD)
-        vt_all[n] = kv_refs[n][:, low + ROWS : low + 2 * ROWS].reshape(TILE, HD).T
-        kz = zp ^ (n & 1)
-        kc = c ^ (n >> 1)
+    halves = 2 * QUADS
+    lane = lax.broadcasted_iota(jnp.int32, (1, HD), 1)
+    row_half = lax.broadcasted_iota(jnp.int32, (TILE, HD), 0) // HALF
+    column = lax.broadcasted_iota(jnp.int32, (TILE, HD), 1)
+    key_half = jnp.full((1, HD), -1, jnp.int32)
+    for n, (low, other_z, other_c) in enumerate(members):
+        k_all[n, :, 0:HD] = kv_refs[n][:, low : low + ROWS].reshape(TILE, HD)
+        k_all[n, :, HD:] = jnp.where(column == n * halves + row_half, 1.0, 0.0).astype(bf16)
+        vt_all[n, 0:HD, :] = kv_refs[n][:, low + ROWS : low + 2 * ROWS].reshape(TILE, HD).T
+        vt_all[n, HD:, :] = jnp.ones((ACC - HD, TILE), bf16)
+        kz = 1 - zp if other_z else zp
+        kc = 1 - c if other_c else c
         for quad in range(QUADS):
-            dev = quad * 16 + kz * 8 + y * 2 + kc
+            dev = kz * 32 + quad * 8 + y * 2 + kc
             for half in range(2):
-                start = order_ref[2 * dev + half] * HALF
-                key_pos[n, pl.ds((quad * 2 + half) * HALF, HALF), :] = (
-                    lax.broadcasted_iota(jnp.int32, (HALF, 128), 0) + start
-                )
-
-    lane = lax.broadcasted_iota(jnp.int32, (1, 128), 1)
-
-    def one_block(qy, carry):
-        pieces = []
+                spot = n * halves + quad * 2 + half
+                key_half = jnp.where(lane == spot, order_ref[2 * dev + half], key_half)
+    below = lax.broadcasted_iota(jnp.int32, (ROWS, ROWS), 0)
+    right = lax.broadcasted_iota(jnp.int32, (ROWS, ROWS), 1)
+    later = (below > right) & (below // HALF == right // HALF)
+
+    for qy in range(YS):
+        bias = []
         for quad in range(QUADS):
-            dev = quad * 16 + zp * 8 + qy * 2 + c
-            first = order_ref[2 * dev] * HALF
-            second = order_ref[2 * dev + 1] * HALF - HALF
-            pieces.append(lane + jnp.where(lane < HALF, first, second))
-        q_blk = q_ref[qy].reshape(TILE, HD)
-        peak = jnp.full((1, TILE), neg_fill, f32)
-        for n in range(4):
-            s = lax.dot_general(
+            dev = zp * 32 + quad * 8 + qy * 2 + c
+            for half in range(2):
+                row = jnp.where(key_half > order_ref[2 * dev + half], neg_fill, 0.0)
+                bias.append(jnp.broadcast_to(row, (HALF, HD)))
+        bias = jnp.concatenate(bias, axis=0).astype(bf16)
+        q_blk = jnp.concatenate([q_ref[qy].reshape(TILE, HD), bias], axis=1)
+        for n in range(count):
+            scores[qy, n] = lax.dot_general(
                 k_all[n], q_blk, (((1,), (1,)), ((), ())), preferred_element_type=f32
             )
-            kp = key_pos[n]
-            cols = []
+        if not resume:
+            own_later = later & (qy == y)
             for quad in range(QUADS):
-                visible = kp <= pieces[quad]
-                cols.append(jnp.where(visible, s[:, quad * 128 : (quad + 1) * 128], neg_fill))
-            s = jnp.concatenate(cols, axis=1)
-            scores[n] = s
-            peak = jnp.maximum(peak, jnp.max(s, axis=0, keepdims=True))
-        total = jnp.zeros((1, TILE), f32)
-        acc = jnp.zeros((HD, TILE), f32)
-        for n in range(4):
-            p = jnp.exp2((scores[n] - peak) * scale2)
-            total = total + jnp.sum(p, axis=0, keepdims=True)
-            acc = acc + jnp.dot(vt_all[n], p.astype(bf16), preferred_element_type=f32)
-        out_ref[qy, 0:HD, :] = acc.astype(bf16)
+                spot = slice(quad * ROWS, (quad + 1) * ROWS)
+                scores[qy, 0, spot, spot] = jnp.where(own_later, neg_fill, scores[qy, 0, spot, spot])
+
+        old = peak_in[qy, 0:1, :] if resume else jnp.full((1, TILE), neg_fill, f32)
+        peak = old
+        for n in range(count):
+            peak = jnp.maximum(peak, jnp.max(scores[qy, n], axis=0, keepdims=True))
+        acc = acc_in[qy] * jnp.exp2((old - peak) * scale2) if resume else jnp.zeros((ACC, TILE), f32)
+        for n in range(count):
+            p = jnp.exp2((scores[qy, n] - peak) * scale2).astype(bf16)
+            acc = acc + jnp.dot(vt_all[n], p, preferred_element_type=f32)
+        if not final:
+            acc_out[qy] = acc
+            peak_out[qy] = jnp.broadcast_to(peak, (8, TILE))
+            continue
+        out_ref[qy, 0:HD, :] = acc[0:HD].astype(bf16)
         rows = []
-        for stat in (peak, total):
+        for stat in (peak, acc[HD : HD + 1]):
             rest = stat
-            for piece in range(3):
+            for _ in range(3):
                 part = rest.astype(bf16).astype(f32)
                 rows.append(part)
                 rest = rest - part
         rows.append(jnp.zeros((STAT_ROWS - 6, TILE), f32))
-        out_ref[qy, HD : HD + STAT_ROWS, :] = jnp.concatenate(rows, axis=0).astype(bf16)
-        return carry
-
-    lax.fori_loop(0, 4, one_block, 0)
-
-
-def attend(where, order, q_all, kv_blocks):
-    return pl.pallas_call(
-        attend_kernel,
-        out_shape=jax.ShapeDtypeStruct((YS, HD + STAT_ROWS, TILE), bf16),
-        in_specs=[smem_spec(), smem_spec()] + [vmem_spec()] * 5,
-        out_specs=vmem_spec(),
+        out_ref[qy, HD:ACC, :] = jnp.concatenate(rows, axis=0).astype(bf16)
+
+
+def attend(where, order, q_all, kv_blocks, members, state=(), final=False):
+    def kernel(*refs):
+        attend_kernel(members, len(state) > 0, final, *refs)
+
+    if final:
+        shape = jax.ShapeDtypeStruct((YS, ACC, TILE), bf16)
+        specs = vmem_spec()
+    else:
+        shape = (
+            jax.ShapeDtypeStruct((YS, ACC, TILE), f32),
+            jax.ShapeDtypeStruct((YS, 8, TILE), f32),
+        )
+        specs = (vmem_spec(), vmem_spec())
+    count = len(members)
+    return pl.pallas_call(
+        kernel,
+        out_shape=shape,
+        in_specs=[smem_spec(), smem_spec()] + [vmem_spec()] * (1 + count + len(state)),
+        out_specs=specs,
         scratch_shapes=[
-            pltpu.VMEM((4, TILE, HD), bf16),
-            pltpu.VMEM((4, HD, TILE), bf16),
-            pltpu.VMEM((4, TILE, TILE), f32),
-            pltpu.VMEM((4, TILE, 128), jnp.int32),
+            pltpu.VMEM((count, TILE, 2 * HD), bf16),
+            pltpu.VMEM((count, ACC, TILE), bf16),
+            pltpu.VMEM((YS, count, TILE, TILE), f32),
         ],
         compiler_params=params(),
         cost_estimate=pl.CostEstimate(
-            flops=4 * 2048 * 2048 * 128, bytes_accessed=2 << 20, transcendentals=1 << 22
+            flops=count * 2048 * 2048 * 128,
+            bytes_accessed=2 << 20,
+            transcendentals=count << 20,
         ),
-        name="attend",
-    )(where, order, q_all, *kv_blocks)
+        name="attend_last" if final else "attend_more" if state else "attend_first",
+    )(where, order, q_all, *kv_blocks, *state)
 
 
 def merge_kernel(part_ref, out_ref):
@@ -339,39 +369,45 @@
     return squares + lax.ppermute(squares, "g", [(i ^ stride, i) for i in range(groups)])
 
 
-def body(
+def everything(
     queries, keys, values, block_order, token_ids, stream_table, short_filter, long_filter, norm_gain
 ):
     groups = lax.axis_size("g")
     zp, y, c = lax.axis_index("zp"), lax.axis_index("y"), lax.axis_index("c")
-    rank = ((lax.axis_index("zq") * 2 + zp) * 4 + y) * 2 + c
+    rank = ((zp * QUADS + lax.axis_index("zq")) * YS + y) * 2 + c
     devices = QUADS * 2 * YS * 2
-
-    own = lax.all_to_all(pack(queries, keys, values), "zq", 0, 0)
 
     near = lax.ppermute(token_ids, CTX, [(i, i + 1) for i in range(devices - 1)])
     far = lax.ppermute(token_ids, CTX, [(i, i + 2) for i in range(devices - 2)])
+    packed = pack(queries, keys, values)
+    packed, near, far = lax.optimization_barrier((packed, near, far))
+    own = lax.all_to_all(packed, "zq", 0, 0)
+
     mixed, squares = hyena(
         rank.reshape(1), far[None], near[None], token_ids[None],
         stream_table, short_filter, long_filter,
     )
-    squares = across(squares, 1)
+    squares = across(squares, 2)
     own, mixed, squares = lax.optimization_barrier((own, mixed, squares))
 
-    q_all = lax.all_to_all(jnp.broadcast_to(own[None, :, 0:ROWS], (YS, QUADS, ROWS, HD)), "y", 0, 0)
     swap = [(0, 1), (1, 0)]
     kv_own = own[:, ROWS:]
     kv_z = lax.ppermute(kv_own, "zp", swap)
+    q_all = jnp.broadcast_to(own[None, :, 0:ROWS], (YS, QUADS, ROWS, HD))
+    q_all = lax.all_to_all(q_all, "y", 0, 0)
     kv_c = lax.ppermute(kv_own, "c", swap)
+    squares = across(squares, 1)
+    where = jnp.stack([zp, y, c])
+    near_members = ((ROWS, False, False), (0, False, True))
+    state = attend(where, block_order, q_all, [own, kv_c], near_members)
+    kv_z, state = lax.optimization_barrier((kv_z, state))
     kv_zc = lax.ppermute(kv_z, "c", swap)
-    where = jnp.stack([zp, y, c])
-    parts = attend(where, block_order, q_all, [own, kv_z, kv_c, kv_zc])
+    state = attend(where, block_order, q_all, [kv_z], ((0, True, False),), state)
+    parts = attend(where, block_order, q_all, [kv_zc], ((0, True, True),), state, True)
     parts, squares = lax.optimization_barrier((parts, squares))
-    parts = lax.all_to_all(parts, "y", 0, 0)
-    for stride in (2, 4):
-        squares = across(squares, stride)
-    parts, squares = lax.optimization_barrier((parts, squares))
-    blocks = lax.all_to_all(merge(parts), "zq", 0, 0)
+    merged = merge(lax.all_to_all(parts, "y", 0, 0))
+    merged, squares = lax.optimization_barrier((merged, across(squares, 4)))
+    blocks = lax.all_to_all(merged, "zq", 0, 0)
     hyena_out = norm(mixed, squares, norm_gain[None], stream_table.shape[2] * groups)
     blocks, hyena_out = lax.optimization_barrier((blocks, hyena_out))
     return (unpack(blocks), hyena_out)
@@ -379,7 +415,7 @@
 
 def solution(mesh):
     groups = mesh.shape["grp"]
-    fine = Mesh(mesh.devices.reshape(QUADS, 2, YS, 2, groups), CTX + ("g",))
+    fine = Mesh(mesh.devices.reshape(2, QUADS, YS, 2, groups), CTX + ("g",))
     placed = (
         P(CTX, "g"),
         P(CTX, "g"),
@@ -392,7 +428,7 @@
         P("g"),
     )
     return jax.shard_map(
-        body,
+        everything,
         mesh=fine,
         in_specs=placed,
         out_specs=(P(CTX, "g"), P(CTX, "g")),

time: 117 us -> 118 us (level)
  the two profiles are of different devices: /device:TPU:14 before, /device:TPU:4 now
where the time goes in v2:
time: 118 us
  starting transfers between devices  55.8 us (47%)
  waiting for transfers between devices  37 us (31%)
  Pallas kernels  22.4 us (19%)
    ppermute x1, waiting for transfers between devices, everything(): kv_z = lax.ppermute(kv_own, 'zp', swap)  19.5 us
    ppermute x3, starting transfers between devices, across(): lax.ppermute(squares, 'g', [(i ^ stride, i) for i in range(groups)])  17 us
    pallas_call x3, Pallas kernels, attend(): pl.pallas_call(kernel, out_shape=shape, in_specs=[smem_spec(), smem_spec(...  10.7 us
    ppermute x3, waiting for transfers between devices, across(): lax.ppermute(squares, 'g', [(i ^ stride, i) for i in range(groups)])  9.64 us
    ppermute x1, starting transfers between devices, everything(): kv_z = lax.ppermute(kv_own, 'zp', swap)  9.1 us
    all_to_all x1, starting transfers between devices, everything(): own = lax.all_to_all(packed, 'zq', 0, 0)  8.24 us
    pallas_call x1, Pallas kernels, hyena(): pl.pallas_call(hyena_kernel, grid=(channels // CHAN_BLOCK,), out_shape=(j...  7.57 us
    all_to_all x1, waiting for transfers between devices, everything(): blocks = lax.all_to_all(merged, 'zq', 0, 0)  5.09 us
  transfers between devices with their start and end apart: 12, of which 6 were waited for; matrix products, arithmetic and copies ran while one was open for 1% of the time, Pallas kernels for 15%

profile of v2, /device:TPU:4, one launch (start us, length us, event | category | flops | bytes accessed | tf_op | source)
XLA Modules:
  0.0 117.7 jit_solution(9168139761267176281)
XLA Ops:
  0.6 1.7 %collective-permute-start = (s32[128]{0:T(128)}, s32[128]{0:T(128)S(1)}, u32[]{:S(2)}, u32[]{:S(2)}) collective-permute-start(s32[128]{0:T(128)} %param.13), channel_id=1, source_target_pairs={{0,8},{8,16},{16,24},{24,32},{32,40},{40,48},{48,56},{56,64},{64,7... | collective-permute-start | bytes 1544 | tf_op jit(solution)/shard_map/ppermute | solution.py:380
  2.4 3.7 %collective-permute-start.1 = (s32[128]{0:T(128)}, s32[128]{0:T(128)S(1)}, u32[]{:S(2)}, u32[]{:S(2)}) collective-permute-start(s32[128]{0:T(128)} %param.13), channel_id=1, source_target_pairs={{0,16},{8,24},{16,32},{24,40},{32,48},{40,56},{48,64},{56,72},{64,... | collective-permute-start | bytes 1544 | tf_op jit(solution)/shard_map/ppermute | solution.py:381
  6.1 1.8 %pack.1 = bf16[4,384,128]{2,1,0:T(8,128)(2,1)} custom-call(bf16[128,512]{1,0:T(8,128)(2,1)} %q_hbm.1, bf16[128,512]{1,0:T(8,128)(2,1)} %k_hbm.1, bf16[128,512]{1,0:T(8,128)(2,1)} %v_hbm.1), custom_call_target="tpu_custom_call" | custom-call | bytes 786432 | tf_op jit(solution)/shard_map/pack/pallas_call | solution.py:54
  7.9 8.2 %all-to-all-start = ((bf16[4,384,128]{2,1,0:T(8,128)(2,1)}), bf16[4,384,128]{2,1,0:T(8,128)(2,1)S(1)}, u32[]{:S(2)}, u32[]{:S(2)}) async-start(bf16[4,384,128]{2,1,0:T(8,128)(2,1)} %pack.1), calls=%async_computation | async-start | bytes 786432 | tf_op jit(solution)/shard_map/all_to_all | solution.py:384
  16.2 7.6 %hyena.1 = (f32[128,1024]{1,0:T(8,128)}, f32[1,128]{1,0:T(1,128)}) custom-call(s32[1]{0:T(128)} %bitcast.3.rank_ref, s32[1,128]{1,0:T(1,128)} %bitcast.11, s32[1,128]{1,0:T(1,128)} %bitcast.10, s32[1,128]{1,0:T(1,128)} %bitcast.9, bf16[4,512,1024]{2,1,0:T(8,128)(2,1)} %table_ref.1, f32[3,7,1024]{2,1,0:T(8,128)} %short_ref.1, bf16[64,128]{1,0:T(8,128)(2,1)} %long_ref.1), custom_call_target="tpu_custom_call" | custom-call | flops 1073741824 | bytes 5242880 | tf_op jit(solution)/shard_map/hyena/pallas_call | solution.py:306
  23.7 3.1 %collective-permute-start.2 = (f32[1,128]{1,0:T(1,128)}, f32[1,128]{1,0:T(1,128)S(1)}, u32[]{:S(2)}, u32[]{:S(2)}) collective-permute-start(f32[1,128]{1,0:T(1,128)} %get-tuple-element.27), channel_id=1, source_target_pairs={{2,0},{3,1},{0,2},{1,3},{6,4},{7,5},{4,6},{5,7},{10,8},{11,9},{8,1... | collective-permute-start | bytes 1544 | tf_op jit(solution)/shard_map/ppermute | solution.py:369
  26.9 2.4 %collective-permute-done.2 = f32[1,128]{1,0:T(1,128)S(1)} collective-permute-done((f32[1,128]{1,0:T(1,128)}, f32[1,128]{1,0:T(1,128)S(1)}, u32[]{:S(2)}, u32[]{:S(2)}) %collective-permute-start.2) | collective-permute-done | bytes 544 | tf_op jit(solution)/shard_map/ppermute | solution.py:369
  29.9 0.9 broadcast_in_dim.21
  30.9 3.5 %all-to-all-start.1 = ((bf16[4,4,128,128]{3,2,1,0:T(8,128)(2,1)}), bf16[4,4,128,128]{3,2,1,0:T(8,128)(2,1)S(1)}, u32[]{:S(2)}, u32[]{:S(2)}) async-start(bf16[4,4,128,128]{3,2,1,0:T(8,128)(2,1)} %broadcast_in_dim.21), calls=%async_computation.1 | async-start | bytes 1048576 | tf_op jit(solution)/shard_map/all_to_all | solution.py:397
  34.4 1.9 %collective-permute-start.4 = (bf16[4,256,128]{2,1,0:T(8,128)(2,1)S(1)}, bf16[4,256,128]{2,1,0:T(8,128)(2,1)S(1)}, u32[]{:S(2)}, u32[]{:S(2)}) collective-permute-start(bf16[4,256,128]{2,1,0:T(8,128)(2,1)S(1)} %slice.7), channel_id=1, source_target_pairs={{0,8},{8,0},{1,9},{9,1},{2,10},{10,2},{3,11},{11,3},{4,12},{12,4},... | collective-permute-start | bytes 786440 | tf_op jit(solution)/shard_map/ppermute | solution.py:398
  36.3 9.1 %collective-permute-start.3 = (bf16[4,256,128]{2,1,0:T(8,128)(2,1)S(1)}, bf16[4,256,128]{2,1,0:T(8,128)(2,1)S(1)}, u32[]{:S(2)}, u32[]{:S(2)}) collective-permute-start(bf16[4,256,128]{2,1,0:T(8,128)(2,1)S(1)} %slice.7), channel_id=1, source_target_pairs={{0,256},{256,0},{1,257},{257,1},{2,258},{258,2},{3,259},{259,3},{4... | collective-permute-start | bytes 786440 | tf_op jit(solution)/shard_map/ppermute | solution.py:395
  45.5 4.2 %attend_first.1 = (f32[4,144,512]{2,1,0:T(8,128)S(1)}, f32[4,8,512]{2,1,0:T(8,128)S(1)}) custom-call(s32[3]{0:T(128)S(1)} %pad_add_fusion.refs_0_, s32[128]{0:T(128)S(1)} %copy-done.2, bf16[4,4,128,128]{3,2,1,0:T(8,128)(2,1)S(1)} %all-to-all-done.1.refs_2_, bf16[4,384,128]{2,1,0:T(8,128)(2,1)S(1)} %all-to-all-done.refs_3_, ...), custom_call_target="tpu_custom_call" | custom-call | flops 1073741824 | bytes 2097152 | tf_op jit(solution)/shard_map/attend_first/pallas_call | solution.py:164
  49.7 19.5 %collective-permute-done.3.refs_3_ = bf16[4,256,128]{2,1,0:T(8,128)(2,1)S(1)} collective-permute-done((bf16[4,256,128]{2,1,0:T(8,128)(2,1)S(1)}, bf16[4,256,128]{2,1,0:T(8,128)(2,1)S(1)}, u32[]{:S(2)}, u32[]{:S(2)}) %collective-permute-start.3) | collective-permute-done | bytes 262176 | tf_op jit(solution)/shard_map/ppermute | solution.py:395
  69.2 1.9 %collective-permute-start.5 = (bf16[4,256,128]{2,1,0:T(8,128)(2,1)S(1)}, bf16[4,256,128]{2,1,0:T(8,128)(2,1)S(1)}, u32[]{:S(2)}, u32[]{:S(2)}) collective-permute-start(bf16[4,256,128]{2,1,0:T(8,128)(2,1)S(1)} %collective-permute-done.3.refs_3_), channel_id=1, source_target_pairs={{0,8},{8,0},{1,9},{9,1},{2,10},{10,2},{3,11},{11,3},{4,12},{12,4},... | collective-permute-start | bytes 786440 | tf_op jit(solution)/shard_map/ppermute | solution.py:404
  71.1 11.5 %collective-permute-start.6 = (f32[1,128]{1,0:T(1,128)S(1)}, f32[1,128]{1,0:T(1,128)S(1)}, u32[]{:S(2)}, u32[]{:S(2)}) collective-permute-start(f32[1,128]{1,0:T(1,128)S(1)} %add.21), channel_id=1, source_target_pairs={{1,0},{0,1},{3,2},{2,3},{5,4},{4,5},{7,6},{6,7},{9,8},{8,9},{11,10... | collective-permute-start | bytes 1544 | tf_op jit(solution)/shard_map/ppermute | solution.py:369
  82.6 2.7 %collective-permute-done.6 = f32[1,128]{1,0:T(1,128)S(1)} collective-permute-done((f32[1,128]{1,0:T(1,128)S(1)}, f32[1,128]{1,0:T(1,128)S(1)}, u32[]{:S(2)}, u32[]{:S(2)}) %collective-permute-start.6) | collective-permute-done | bytes 544 | tf_op jit(solution)/shard_map/ppermute | solution.py:369
  85.3 2.8 %attend_more.1 = (f32[4,144,512]{2,1,0:T(8,128)S(1)}, f32[4,8,512]{2,1,0:T(8,128)S(1)}) custom-call(s32[3]{0:T(128)S(1)} %pad_add_fusion.refs_0_, s32[128]{0:T(128)S(1)} %copy-done.2, bf16[4,4,128,128]{3,2,1,0:T(8,128)(2,1)S(1)} %all-to-all-done.1.refs_2_, bf16[4,256,128]{2,1,0:T(8,128)(2,1)S(1)} %collective-permute-done.3.refs_3_, ...), custom_call_target="tpu_custom_call" | custom-call | flops 536870912 | bytes 2097152 | tf_op jit(solution)/shard_map/attend_more/pallas_call | solution.py:164
  88.1 3.7 %attend_last.1 = bf16[4,144,512]{2,1,0:T(8,128)(2,1)} custom-call(s32[3]{0:T(128)S(1)} %pad_add_fusion.refs_0_, s32[128]{0:T(128)S(1)} %copy-done.2, bf16[4,4,128,128]{3,2,1,0:T(8,128)(2,1)S(1)} %all-to-all-done.1.refs_2_, bf16[4,256,128]{2,1,0:T(8,128)(2,1)S(1)} %collective-permute-done.5.refs_3_, f32[4,144,512]{2,1,0:T(8,128)S(1)} %get-tuple-element.34.refs_4_, ...), custom_call_target="tpu_custom_call" | custom-call | flops 536870912 | bytes 2097152 | tf_op jit(solution)/shard_map/attend_last/pallas_call | solution.py:164
  91.8 4.9 %all-to-all-start.2 = ((bf16[4,144,512]{2,1,0:T(8,128)(2,1)}), bf16[4,144,512]{2,1,0:T(8,128)(2,1)S(1)}, u32[]{:S(2)}, u32[]{:S(2)}) async-start(bf16[4,144,512]{2,1,0:T(8,128)(2,1)} %attend_last.1), calls=%async_computation.2 | async-start | bytes 1179648 | tf_op jit(solution)/shard_map/all_to_all | solution.py:408
  96.7 2.4 %collective-permute-start.7 = (f32[1,128]{1,0:T(1,128)S(1)}, f32[1,128]{1,0:T(1,128)S(1)}, u32[]{:S(2)}, u32[]{:S(2)}) collective-permute-start(f32[1,128]{1,0:T(1,128)S(1)} %add.22), channel_id=1, source_target_pairs={{4,0},{5,1},{6,2},{7,3},{0,4},{1,5},{2,6},{3,7},{12,8},{13,9},{14,... | collective-permute-start | bytes 1544 | tf_op jit(solution)/shard_map/ppermute | solution.py:369
  99.1 4.5 %collective-permute-done.7 = f32[1,128]{1,0:T(1,128)S(1)} collective-permute-done((f32[1,128]{1,0:T(1,128)S(1)}, f32[1,128]{1,0:T(1,128)S(1)}, u32[]{:S(2)}, u32[]{:S(2)}) %collective-permute-start.7) | collective-permute-done | bytes 544 | tf_op jit(solution)/shard_map/ppermute | solution.py:369
  103.7 2.7 %all-to-all-done.2.part_ref = bf16[4,144,512]{2,1,0:T(8,128)(2,1)S(1)} async-done(((bf16[4,144,512]{2,1,0:T(8,128)(2,1)}), bf16[4,144,512]{2,1,0:T(8,128)(2,1)S(1)}, u32[]{:S(2)}, u32[]{:S(2)}) %all-to-all-start.2) | async-done | bytes 589856 | tf_op jit(solution)/shard_map/all_to_all | solution.py:408
  107.3 3.8 %all-to-all-start.3 = ((bf16[4,128,128]{2,1,0:T(8,128)(2,1)}), bf16[4,128,128]{2,1,0:T(8,128)(2,1)S(1)}, u32[]{:S(2)}, u32[]{:S(2)}) async-start(bf16[4,128,128]{2,1,0:T(8,128)(2,1)} %merge.1), calls=%async_computation.3 | async-start | bytes 262144 | tf_op jit(solution)/shard_map/all_to_all | solution.py:410
  111.9 5.1 %all-to-all-done.3.x_ref = bf16[4,128,128]{2,1,0:T(8,128)(2,1)S(1)} async-done(((bf16[4,128,128]{2,1,0:T(8,128)(2,1)}), bf16[4,128,128]{2,1,0:T(8,128)(2,1)S(1)}, u32[]{:S(2)}, u32[]{:S(2)}) %all-to-all-start.3) | async-done | bytes 131104 | tf_op jit(solution)/shard_map/all_to_all | solution.py:410
  (25 shorter events, 3.2 us)
Async XLA Ops:
  0.6 7.3 %collective-permute-start = (s32[128]{0:T(128)}, s32[128]{0:T(128)S(1)}, u32[]{:S(2)}, u32[]{:S(2)}) collective-permute-start(s32[128]{0:T(128)} %param.13), channel_id=1, source_target_pairs={{0,8},{8,16},{16,24},{24,32},{32,40},{40,48},{48,56},{56,64},{64,7... | collective-permute-start | bytes 1544 | tf_op jit(solution)/shard_map/ppermute | solution.py:380
  2.4 5.5 %collective-permute-start.1 = (s32[128]{0:T(128)}, s32[128]{0:T(128)S(1)}, u32[]{:S(2)}, u32[]{:S(2)}) collective-permute-start(s32[128]{0:T(128)} %param.13), channel_id=1, source_target_pairs={{0,16},{8,24},{16,32},{24,40},{32,48},{40,56},{48,64},{56,72},{64,... | collective-permute-start | bytes 1544 | tf_op jit(solution)/shard_map/ppermute | solution.py:381
  7.9 8.3 %copy-start.3 = (s32[128]{0:T(128)}, s32[128]{0:T(128)S(1)}, u32[]{:S(2)}) copy-start(s32[128]{0:T(128)S(1)} %collective-permute-done) | copy-start | bytes 1540
  7.9 8.3 %copy-start.4 = (s32[128]{0:T(128)}, s32[128]{0:T(128)S(1)}, u32[]{:S(2)}) copy-start(s32[128]{0:T(128)S(1)} %collective-permute-done.1) | copy-start | bytes 1540
  7.9 22.0 %all-to-all-start = ((bf16[4,384,128]{2,1,0:T(8,128)(2,1)}), bf16[4,384,128]{2,1,0:T(8,128)(2,1)S(1)}, u32[]{:S(2)}, u32[]{:S(2)}) async-start(bf16[4,384,128]{2,1,0:T(8,128)(2,1)} %pack.1), calls=%async_computation | async-start | bytes 786432 | tf_op jit(solution)/shard_map/all_to_all | solution.py:384
  23.7 5.5 %collective-permute-start.2 = (f32[1,128]{1,0:T(1,128)}, f32[1,128]{1,0:T(1,128)S(1)}, u32[]{:S(2)}, u32[]{:S(2)}) collective-permute-start(f32[1,128]{1,0:T(1,128)} %get-tuple-element.27), channel_id=1, source_target_pairs={{2,0},{3,1},{0,2},{1,3},{6,4},{7,5},{4,6},{5,7},{10,8},{11,9},{8,1... | collective-permute-start | bytes 1544 | tf_op jit(solution)/shard_map/ppermute | solution.py:369
  29.9 15.5 %copy-start.2 = (s32[128]{0:T(128)S(1)}, s32[128]{0:T(128)}, u32[]{:S(2)}) copy-start(s32[128]{0:T(128)} %refs_1_.5) | copy-start | bytes 1540
  30.9 14.6 %all-to-all-start.1 = ((bf16[4,4,128,128]{3,2,1,0:T(8,128)(2,1)}), bf16[4,4,128,128]{3,2,1,0:T(8,128)(2,1)S(1)}, u32[]{:S(2)}, u32[]{:S(2)}) async-start(bf16[4,4,128,128]{3,2,1,0:T(8,128)(2,1)} %broadcast_in_dim.21), calls=%async_computation.1 | async-start | bytes 1048576 | tf_op jit(solution)/shard_map/all_to_all | solution.py:397
  34.4 11.1 %collective-permute-start.4 = (bf16[4,256,128]{2,1,0:T(8,128)(2,1)S(1)}, bf16[4,256,128]{2,1,0:T(8,128)(2,1)S(1)}, u32[]{:S(2)}, u32[]{:S(2)}) collective-permute-start(bf16[4,256,128]{2,1,0:T(8,128)(2,1)S(1)} %slice.7), channel_id=1, source_target_pairs={{0,8},{8,0},{1,9},{9,1},{2,10},{10,2},{3,11},{11,3},{4,12},{12,4},... | collective-permute-start | bytes 786440 | tf_op jit(solution)/shard_map/ppermute | solution.py:398
  36.3 32.9 %collective-permute-start.3 = (bf16[4,256,128]{2,1,0:T(8,128)(2,1)S(1)}, bf16[4,256,128]{2,1,0:T(8,128)(2,1)S(1)}, u32[]{:S(2)}, u32[]{:S(2)}) collective-permute-start(bf16[4,256,128]{2,1,0:T(8,128)(2,1)S(1)} %slice.7), channel_id=1, source_target_pairs={{0,256},{256,0},{1,257},{257,1},{2,258},{258,2},{3,259},{259,3},{4... | collective-permute-start | bytes 786440 | tf_op jit(solution)/shard_map/ppermute | solution.py:395
  69.2 18.9 %collective-permute-start.5 = (bf16[4,256,128]{2,1,0:T(8,128)(2,1)S(1)}, bf16[4,256,128]{2,1,0:T(8,128)(2,1)S(1)}, u32[]{:S(2)}, u32[]{:S(2)}) collective-permute-start(bf16[4,256,128]{2,1,0:T(8,128)(2,1)S(1)} %collective-permute-done.3.refs_3_), channel_id=1, source_target_pairs={{0,8},{8,0},{1,9},{9,1},{2,10},{10,2},{3,11},{11,3},{4,12},{12,4},... | collective-permute-start | bytes 786440 | tf_op jit(solution)/shard_map/ppermute | solution.py:404
  71.1 14.2 %collective-permute-start.6 = (f32[1,128]{1,0:T(1,128)S(1)}, f32[1,128]{1,0:T(1,128)S(1)}, u32[]{:S(2)}, u32[]{:S(2)}) collective-permute-start(f32[1,128]{1,0:T(1,128)S(1)} %add.21), channel_id=1, source_target_pairs={{1,0},{0,1},{3,2},{2,3},{5,4},{4,5},{7,6},{6,7},{9,8},{8,9},{11,10... | collective-permute-start | bytes 1544 | tf_op jit(solution)/shard_map/ppermute | solution.py:369
  91.8 19.3 %copy-start = (f32[128,1024]{1,0:T(8,128)S(1)}, f32[128,1024]{1,0:T(8,128)}, u32[]{:S(2)}) copy-start(f32[128,1024]{1,0:T(8,128)} %get-tuple-element.40.refs_0_) | copy-start | bytes 1572868
  91.8 19.3 %copy-start.1 = (f32[1024]{0:T(1024)S(1)}, f32[1024]{0:T(1024)}, u32[]{:S(2)}) copy-start(f32[1024]{0:T(1024)} %param.17) | copy-start | bytes 12292
  91.8 14.6 %all-to-all-start.2 = ((bf16[4,144,512]{2,1,0:T(8,128)(2,1)}), bf16[4,144,512]{2,1,0:T(8,128)(2,1)S(1)}, u32[]{:S(2)}, u32[]{:S(2)}) async-start(bf16[4,144,512]{2,1,0:T(8,128)(2,1)} %attend_last.1), calls=%async_computation.2 | async-start | bytes 1179648 | tf_op jit(solution)/shard_map/all_to_all | solution.py:408
  96.7 7.0 %collective-permute-start.7 = (f32[1,128]{1,0:T(1,128)S(1)}, f32[1,128]{1,0:T(1,128)S(1)}, u32[]{:S(2)}, u32[]{:S(2)}) collective-permute-start(f32[1,128]{1,0:T(1,128)S(1)} %add.22), channel_id=1, source_target_pairs={{4,0},{5,1},{6,2},{7,3},{0,4},{1,5},{2,6},{3,7},{12,8},{13,9},{14,... | collective-permute-start | bytes 1544 | tf_op jit(solution)/shard_map/ppermute | solution.py:369
  107.3 9.7 %all-to-all-start.3 = ((bf16[4,128,128]{2,1,0:T(8,128)(2,1)}), bf16[4,128,128]{2,1,0:T(8,128)(2,1)S(1)}, u32[]{:S(2)}, u32[]{:S(2)}) async-start(bf16[4,128,128]{2,1,0:T(8,128)(2,1)} %merge.1), calls=%async_computation.3 | async-start | bytes 262144 | tf_op jit(solution)/shard_map/all_to_all | solution.py:410

commit v3 on v2

--- a/solution.py
+++ b/solution.py
@@ -25,6 +25,7 @@
 f32 = jnp.float32
 bf16 = jnp.bfloat16
 CTX = ("zp", "zq", "y", "c")
+GRP = ("x", "zh")
 
 
 def vmem_spec():
@@ -39,15 +40,21 @@
     return pltpu.CompilerParams(vmem_limit_bytes=48 * 1024 * 1024, **kw)
 
 
-def pack_kernel(q_hbm, k_hbm, v_hbm, out_ref, buf, sems):
-    copies = []
+def pack_kernel(q_hbm, k_hbm, v_hbm, out_hbm, buf, out, sems, out_sems):
+    loads = []
     for n, ref in enumerate((q_hbm, k_hbm, v_hbm)):
-        copies.append(pltpu.make_async_copy(ref, buf.at[n], sems.at[n]))
-        copies[-1].start()
-    for n, copy in enumerate(copies):
-        copy.wait()
+        loads.append(pltpu.make_async_copy(ref, buf.at[n], sems.at[n]))
+        loads[-1].start()
+    stores = []
+    for n in range(3):
+        loads[n].wait()
+        rows = slice(n * ROWS, (n + 1) * ROWS)
         for head in range(QUADS):
-            out_ref[head, n * ROWS : (n + 1) * ROWS] = buf[n, :, head * HD : (head + 1) * HD]
+            out[n, head] = buf[n, :, head * HD : (head + 1) * HD]
+        stores.append(pltpu.make_async_copy(out.at[n], out_hbm.at[:, rows], out_sems.at[n]))
+        stores[-1].start()
+    for store in stores:
+        store.wait()
 
 
 def pack(queries, keys, values):
@@ -55,9 +62,11 @@
         pack_kernel,
         out_shape=jax.ShapeDtypeStruct((QUADS, 3 * ROWS, HD), bf16),
         in_specs=[pl.BlockSpec(memory_space=pl.ANY)] * 3,
-        out_specs=vmem_spec(),
+        out_specs=pl.BlockSpec(memory_space=pl.ANY),
         scratch_shapes=[
             pltpu.VMEM((3,) + queries.shape, bf16),
+            pltpu.VMEM((3, QUADS, ROWS, HD), bf16),
+            pltpu.SemaphoreType.DMA((3,)),
             pltpu.SemaphoreType.DMA((3,)),
         ],
         compiler_params=pltpu.CompilerParams(vmem_limit_bytes=60 * 1024 * 1024),
@@ -78,7 +87,8 @@
     if resume:
         acc_in, peak_in, *refs = refs
     if final:
-        out_ref, k_all, vt_all, scores = refs
+        out_hbm, k_all, vt_all, scores, out_ref, out_sems = refs
+        stores = []
     else:
         acc_out, peak_out, k_all, vt_all, scores = refs
     zp, y, c = where_ref[0], where_ref[1], where_ref[2]
@@ -145,6 +155,11 @@
                 rest = rest - part
         rows.append(jnp.zeros((STAT_ROWS - 6, TILE), f32))
         out_ref[qy, HD:ACC, :] = jnp.concatenate(rows, axis=0).astype(bf16)
+        stores.append(pltpu.make_async_copy(out_ref.at[qy], out_hbm.at[qy], out_sems.at[qy]))
+        stores[-1].start()
+    if final:
+        for store in stores:
+            store.wait()
 
 
 def attend(where, order, q_all, kv_blocks, members, state=(), final=False):
@@ -153,13 +168,15 @@
 
     if final:
         shape = jax.ShapeDtypeStruct((YS, ACC, TILE), bf16)
-        specs = vmem_spec()
+        specs = pl.BlockSpec(memory_space=pl.ANY)
+        extra = [pltpu.VMEM((YS, ACC, TILE), bf16), pltpu.SemaphoreType.DMA((YS,))]
     else:
         shape = (
             jax.ShapeDtypeStruct((YS, ACC, TILE), f32),
             jax.ShapeDtypeStruct((YS, 8, TILE), f32),
         )
         specs = (vmem_spec(), vmem_spec())
+        extra = []
     count = len(members)
     return pl.pallas_call(
         kernel,
@@ -170,7 +187,8 @@
             pltpu.VMEM((count, TILE, 2 * HD), bf16),
             pltpu.VMEM((count, ACC, TILE), bf16),
             pltpu.VMEM((YS, count, TILE, TILE), f32),
-        ],
+        ]
+        + extra,
         compiler_params=params(),
         cost_estimate=pl.CostEstimate(
             flops=count * 2048 * 2048 * 128,
@@ -339,40 +357,40 @@
     )(rank, far, near, own, table, short_filter, long_filter)
 
 
-def norm_kernel(channels, mixed_ref, squares_ref, gain_ref, out_ref):
-    mean = squares_ref[...] / channels
+def norm_kernel(channels, mixed_ref, squares_ref, other_ref, gain_ref, out_ref):
+    mean = (squares_ref[...] + other_ref[...]) / channels
     inverse = jnp.broadcast_to(lax.rsqrt(mean + eps_norm), (ROWS, ROWS)).T
     for lb in range(mixed_ref.shape[1] // 128):
         lanes = slice(lb * 128, (lb + 1) * 128)
         out_ref[:, lanes] = (mixed_ref[:, lanes] * gain_ref[:, lanes] * inverse).astype(bf16)
 
 
-def norm(mixed, squares, gain, channels):
+def norm(mixed, squares, other, gain, channels):
     def kernel(*refs):
         norm_kernel(channels, *refs)
 
     return pl.pallas_call(
         kernel,
         out_shape=jax.ShapeDtypeStruct(mixed.shape, bf16),
-        in_specs=[vmem_spec()] * 3,
+        in_specs=[vmem_spec()] * 4,
         out_specs=vmem_spec(),
         compiler_params=params(),
         cost_estimate=pl.CostEstimate(flops=1 << 18, bytes_accessed=800000, transcendentals=128),
         name="norm",
-    )(mixed, squares, gain)
+    )(mixed, squares, other, gain)
 
 
 def across(squares, stride):
-    groups = lax.axis_size("g")
-    if stride >= groups:
-        return squares
-    return squares + lax.ppermute(squares, "g", [(i ^ stride, i) for i in range(groups)])
+    members = lax.axis_size("x")
+    if stride >= members:
+        return jnp.zeros_like(squares)
+    return lax.ppermute(squares, "x", [(i ^ stride, i) for i in range(members)])
 
 
 def everything(
     queries, keys, values, block_order, token_ids, stream_table, short_filter, long_filter, norm_gain
 ):
-    groups = lax.axis_size("g")
+    groups = lax.axis_size(("x", "zh"))
     zp, y, c = lax.axis_index("zp"), lax.axis_index("y"), lax.axis_index("c")
     rank = ((zp * QUADS + lax.axis_index("zq")) * YS + y) * 2 + c
     devices = QUADS * 2 * YS * 2
@@ -380,14 +398,12 @@
     near = lax.ppermute(token_ids, CTX, [(i, i + 1) for i in range(devices - 1)])
     far = lax.ppermute(token_ids, CTX, [(i, i + 2) for i in range(devices - 2)])
     packed = pack(queries, keys, values)
-    packed, near, far = lax.optimization_barrier((packed, near, far))
     own = lax.all_to_all(packed, "zq", 0, 0)
 
     mixed, squares = hyena(
         rank.reshape(1), far[None], near[None], token_ids[None],
         stream_table, short_filter, long_filter,
     )
-    squares = across(squares, 2)
     own, mixed, squares = lax.optimization_barrier((own, mixed, squares))
 
     swap = [(0, 1), (1, 0)]
@@ -396,41 +412,45 @@
     q_all = jnp.broadcast_to(own[None, :, 0:ROWS], (YS, QUADS, ROWS, HD))
     q_all = lax.all_to_all(q_all, "y", 0, 0)
     kv_c = lax.ppermute(kv_own, "c", swap)
-    squares = across(squares, 1)
     where = jnp.stack([zp, y, c])
+    other = lax.ppermute(squares, "zh", swap)
     near_members = ((ROWS, False, False), (0, False, True))
     state = attend(where, block_order, q_all, [own, kv_c], near_members)
     kv_z, state = lax.optimization_barrier((kv_z, state))
     kv_zc = lax.ppermute(kv_z, "c", swap)
     state = attend(where, block_order, q_all, [kv_z], ((0, True, False),), state)
     parts = attend(where, block_order, q_all, [kv_zc], ((0, True, True),), state, True)
-    parts, squares = lax.optimization_barrier((parts, squares))
-    merged = merge(lax.all_to_all(parts, "y", 0, 0))
-    merged, squares = lax.optimization_barrier((merged, across(squares, 4)))
+    parts, squares, other = lax.optimization_barrier((parts, squares, other))
+    merged = lax.all_to_all(parts, "y", 0, 0)
+    squares = squares + other
+    squares = squares + across(squares, 2)
+    merged, squares = lax.optimization_barrier((merged, squares))
+    merged = merge(merged)
     blocks = lax.all_to_all(merged, "zq", 0, 0)
-    hyena_out = norm(mixed, squares, norm_gain[None], stream_table.shape[2] * groups)
+    other = across(squares, 1)
+    hyena_out = norm(mixed, squares, other, norm_gain[None], stream_table.shape[2] * groups)
     blocks, hyena_out = lax.optimization_barrier((blocks, hyena_out))
     return (unpack(blocks), hyena_out)
 
 
 def solution(mesh):
     groups = mesh.shape["grp"]
-    fine = Mesh(mesh.devices.reshape(2, QUADS, YS, 2, groups), CTX + ("g",))
+    fine = Mesh(mesh.devices.reshape(2, QUADS, YS, 2, groups // 2, 2), CTX + GRP)
     placed = (
-        P(CTX, "g"),
-        P(CTX, "g"),
-        P(CTX, "g"),
+        P(CTX, GRP),
+        P(CTX, GRP),
+        P(CTX, GRP),
         P(),
         P(CTX),
-        P(None, None, "g"),
-        P(None, None, "g"),
-        P("g", None),
-        P("g"),
+        P(None, None, GRP),
+        P(None, None, GRP),
+        P(GRP, None),
+        P(GRP),
     )
     return jax.shard_map(
         everything,
         mesh=fine,
         in_specs=placed,
-        out_specs=(P(CTX, "g"), P(CTX, "g")),
+        out_specs=(P(CTX, GRP), P(CTX, GRP)),
         check_vma=False,
     )

time: 118 us -> 112 us (0.949)
  the two profiles are of different devices: /device:TPU:4 before, /device:TPU:1 now
where the time goes in v3:
time: 112 us; the launch traced here: 111 us
  starting transfers between devices  59.8 us (53%)
  waiting for transfers between devices  26.2 us (23%)
  Pallas kernels  22.2 us (20%)
  local copies, waits for them, and re-layouts  1.5 us (1%)
    ppermute x1, waiting for transfers between devices, everything(): kv_z = lax.ppermute(kv_own, 'zp', swap)  19.2 us
    pallas_call x3, Pallas kernels, attend(): pl.pallas_call(kernel, out_shape=shape, in_specs=[smem_spec(), smem_spec(...  10.6 us
    ppermute x1, starting transfers between devices, everything(): other = lax.ppermute(squares, 'zh', swap)  9.02 us
    ppermute x1, starting transfers between devices, everything(): kv_z = lax.ppermute(kv_own, 'zp', swap)  8.35 us
    ppermute x2, starting transfers between devices, across(): return lax.ppermute(squares, 'x', [(i ^ stride, i) for i in range(members)])  7.75 us
    pallas_call x1, Pallas kernels, hyena(): pl.pallas_call(hyena_kernel, grid=(channels // CHAN_BLOCK,), out_shape=(j...  7.55 us
    all_to_all x1, starting transfers between devices, everything(): q_all = lax.all_to_all(q_all, 'y', 0, 0)  6.87 us
    all_to_all x1, starting transfers between devices, everything(): own = lax.all_to_all(packed, 'zq', 0, 0)  6.44 us
  transfers between devices with their start and end apart: 12, of which 5 were waited for; matrix products, arithmetic and copies ran while one was open for 0% of the time, Pallas kernels for 17%

profile of v3, /device:TPU:1, one launch (start us, length us, event | category | flops | bytes accessed | tf_op | source)
XLA Modules:
  0.0 110.7 jit_solution(10053324903830461069)
XLA Ops:
  0.6 1.8 %pack.1 = bf16[4,384,128]{2,1,0:T(8,128)(2,1)} custom-call(bf16[128,512]{1,0:T(8,128)(2,1)} %q_hbm.1, bf16[128,512]{1,0:T(8,128)(2,1)} %k_hbm.1, bf16[128,512]{1,0:T(8,128)(2,1)} %v_hbm.1), custom_call_target="tpu_custom_call" | custom-call | bytes 786432 | tf_op jit(solution)/shard_map/pack/pallas_call | solution.py:61
  2.4 6.4 %all-to-all-start = ((bf16[4,384,128]{2,1,0:T(8,128)(2,1)}), bf16[4,384,128]{2,1,0:T(8,128)(2,1)S(1)}, u32[]{:S(2)}, u32[]{:S(2)}) async-start(bf16[4,384,128]{2,1,0:T(8,128)(2,1)} %pack.1), calls=%async_computation | async-start | bytes 786432 | tf_op jit(solution)/shard_map/all_to_all | solution.py:401
  8.9 3.2 %collective-permute-start = (s32[128]{0:T(128)S(1)}, s32[128]{0:T(128)S(1)}, u32[]{:S(2)}, u32[]{:S(2)}) collective-permute-start(s32[128]{0:T(128)S(1)} %copy-done.3), channel_id=1, source_target_pairs={{0,16},{8,24},{16,32},{24,40},{32,48},{40,56},{48,64},{56,72},{64,... | collective-permute-start | bytes 1544 | tf_op jit(solution)/shard_map/ppermute | solution.py:399
  12.0 4.3 %collective-permute-start.1 = (s32[128]{0:T(128)S(1)}, s32[128]{0:T(128)S(1)}, u32[]{:S(2)}, u32[]{:S(2)}) collective-permute-start(s32[128]{0:T(128)S(1)} %copy-done.3), channel_id=1, source_target_pairs={{0,8},{8,16},{16,24},{24,32},{32,40},{40,48},{48,56},{56,64},{64,7... | collective-permute-start | bytes 1544 | tf_op jit(solution)/shard_map/ppermute | solution.py:398
  17.6 7.5 %hyena.1 = (f32[128,1024]{1,0:T(8,128)}, f32[1,128]{1,0:T(1,128)}) custom-call(s32[1]{0:T(128)} %bitcast.3.rank_ref, s32[1,128]{1,0:T(1,128)} %bitcast.10, s32[1,128]{1,0:T(1,128)} %bitcast.11, s32[1,128]{1,0:T(1,128)} %bitcast.9, bf16[4,512,1024]{2,1,0:T(8,128)(2,1)} %table_ref.1, f32[3,7,1024]{2,1,0:T(8,128)} %short_ref.1, bf16[64,128]{1,0:T(8,128)(2,1)} %long_ref.1), custom_call_target="tpu_custom_call" | custom-call | flops 1073741824 | bytes 5242880 | tf_op jit(solution)/shard_map/hyena/pallas_call | solution.py:324
  25.2 0.9 broadcast_in_dim.21
  26.1 6.9 %all-to-all-start.1 = ((bf16[4,4,128,128]{3,2,1,0:T(8,128)(2,1)}), bf16[4,4,128,128]{3,2,1,0:T(8,128)(2,1)S(1)}, u32[]{:S(2)}, u32[]{:S(2)}) async-start(bf16[4,4,128,128]{3,2,1,0:T(8,128)(2,1)} %broadcast_in_dim.21), calls=%async_computation.1 | async-start | bytes 1048576 | tf_op jit(solution)/shard_map/all_to_all | solution.py:413
  33.0 3.4 %collective-permute-start.3 = (bf16[4,256,128]{2,1,0:T(8,128)(2,1)S(1)}, bf16[4,256,128]{2,1,0:T(8,128)(2,1)S(1)}, u32[]{:S(2)}, u32[]{:S(2)}) collective-permute-start(bf16[4,256,128]{2,1,0:T(8,128)(2,1)S(1)} %slice.7), channel_id=1, source_target_pairs={{0,8},{8,0},{1,9},{9,1},{2,10},{10,2},{3,11},{11,3},{4,12},{12,4},... | collective-permute-start | bytes 786440 | tf_op jit(solution)/shard_map/ppermute | solution.py:414
  36.4 8.3 %collective-permute-start.2 = (bf16[4,256,128]{2,1,0:T(8,128)(2,1)S(1)}, bf16[4,256,128]{2,1,0:T(8,128)(2,1)S(1)}, u32[]{:S(2)}, u32[]{:S(2)}) collective-permute-start(bf16[4,256,128]{2,1,0:T(8,128)(2,1)S(1)} %slice.7), channel_id=1, source_target_pairs={{0,256},{256,0},{1,257},{257,1},{2,258},{258,2},{3,259},{259,3},{4... | collective-permute-start | bytes 786440 | tf_op jit(solution)/shard_map/ppermute | solution.py:411
  44.9 4.2 %attend_first.1 = (f32[4,144,512]{2,1,0:T(8,128)S(1)}, f32[4,8,512]{2,1,0:T(8,128)S(1)}) custom-call(s32[3]{0:T(128)S(1)} %pad_add_fusion.refs_0_, s32[128]{0:T(128)S(1)} %copy-done.2, bf16[4,4,128,128]{3,2,1,0:T(8,128)(2,1)S(1)} %all-to-all-done.1.refs_2_, bf16[4,384,128]{2,1,0:T(8,128)(2,1)S(1)} %all-to-all-done.refs_3_, ...), custom_call_target="tpu_custom_call" | custom-call | flops 1073741824 | bytes 2097152 | tf_op jit(solution)/shard_map/attend_first/pallas_call | solution.py:181
  49.0 19.2 %collective-permute-done.2.refs_3_ = bf16[4,256,128]{2,1,0:T(8,128)(2,1)S(1)} collective-permute-done((bf16[4,256,128]{2,1,0:T(8,128)(2,1)S(1)}, bf16[4,256,128]{2,1,0:T(8,128)(2,1)S(1)}, u32[]{:S(2)}, u32[]{:S(2)}) %collective-permute-start.2) | collective-permute-done | bytes 262176 | tf_op jit(solution)/shard_map/ppermute | solution.py:411
  68.3 2.5 %collective-permute-start.4 = (bf16[4,256,128]{2,1,0:T(8,128)(2,1)S(1)}, bf16[4,256,128]{2,1,0:T(8,128)(2,1)S(1)}, u32[]{:S(2)}, u32[]{:S(2)}) collective-permute-start(bf16[4,256,128]{2,1,0:T(8,128)(2,1)S(1)} %collective-permute-done.2.refs_3_), channel_id=1, source_target_pairs={{0,8},{8,0},{1,9},{9,1},{2,10},{10,2},{3,11},{11,3},{4,12},{12,4},... | collective-permute-start | bytes 786440 | tf_op jit(solution)/shard_map/ppermute | solution.py:420
  70.8 9.0 %collective-permute-start.5 = (f32[1,128]{1,0:T(1,128)S(1)}, f32[1,128]{1,0:T(1,128)S(1)}, u32[]{:S(2)}, u32[]{:S(2)}) collective-permute-start(f32[1,128]{1,0:T(1,128)S(1)} %copy-done.6), channel_id=1, source_target_pairs={{0,1},{1,0},{2,3},{3,2},{4,5},{5,4},{6,7},{7,6},{8,9},{9,8},{10,11... | collective-permute-start | bytes 1544 | tf_op jit(solution)/shard_map/ppermute | solution.py:416
  79.8 2.9 %attend_more.1 = (f32[4,144,512]{2,1,0:T(8,128)S(1)}, f32[4,8,512]{2,1,0:T(8,128)S(1)}) custom-call(s32[3]{0:T(128)S(1)} %pad_add_fusion.refs_0_, s32[128]{0:T(128)S(1)} %copy-done.2, bf16[4,4,128,128]{3,2,1,0:T(8,128)(2,1)S(1)} %all-to-all-done.1.refs_2_, bf16[4,256,128]{2,1,0:T(8,128)(2,1)S(1)} %collective-permute-done.2.refs_3_, ...), custom_call_target="tpu_custom_call" | custom-call | flops 536870912 | bytes 2097152 | tf_op jit(solution)/shard_map/attend_more/pallas_call | solution.py:181
  82.7 3.6 %attend_last.1 = bf16[4,144,512]{2,1,0:T(8,128)(2,1)} custom-call(s32[3]{0:T(128)S(1)} %pad_add_fusion.refs_0_, s32[128]{0:T(128)S(1)} %copy-done.2, bf16[4,4,128,128]{3,2,1,0:T(8,128)(2,1)S(1)} %all-to-all-done.1.refs_2_, bf16[4,256,128]{2,1,0:T(8,128)(2,1)S(1)} %collective-permute-done.4.refs_3_, f32[4,144,512]{2,1,0:T(8,128)S(1)} %get-tuple-element.29.refs_4_, ...), custom_call_target="tpu_custom_call" | custom-call | flops 536870912 | bytes 2097152 | tf_op jit(solution)/shard_map/attend_last/pallas_call | solution.py:181
  86.3 4.7 %all-to-all-start.2 = ((bf16[4,144,512]{2,1,0:T(8,128)(2,1)}), bf16[4,144,512]{2,1,0:T(8,128)(2,1)S(1)}, u32[]{:S(2)}, u32[]{:S(2)}) async-start(bf16[4,144,512]{2,1,0:T(8,128)(2,1)} %attend_last.1), calls=%async_computation.2 | async-start | bytes 1179648 | tf_op jit(solution)/shard_map/all_to_all | solution.py:424
  90.9 4.6 %collective-permute-start.6 = (f32[1,128]{1,0:T(1,128)S(1)}, f32[1,128]{1,0:T(1,128)S(1)}, u32[]{:S(2)}, u32[]{:S(2)}) collective-permute-start(f32[1,128]{1,0:T(1,128)S(1)} %add.18), channel_id=1, source_target_pairs={{4,0},{6,2},{0,4},{2,6},{5,1},{7,3},{1,5},{3,7},{12,8},{14,10},{8,... | collective-permute-start | bytes 1544 | tf_op jit(solution)/shard_map/ppermute | solution.py:387
  95.6 1.2 %collective-permute-done.6 = f32[1,128]{1,0:T(1,128)S(1)} collective-permute-done((f32[1,128]{1,0:T(1,128)S(1)}, f32[1,128]{1,0:T(1,128)S(1)}, u32[]{:S(2)}, u32[]{:S(2)}) %collective-permute-start.6) | collective-permute-done | bytes 544 | tf_op jit(solution)/shard_map/ppermute | solution.py:387
  96.7 3.9 %all-to-all-done.2.part_ref = bf16[4,144,512]{2,1,0:T(8,128)(2,1)S(1)} async-done(((bf16[4,144,512]{2,1,0:T(8,128)(2,1)}), bf16[4,144,512]{2,1,0:T(8,128)(2,1)S(1)}, u32[]{:S(2)}, u32[]{:S(2)}) %all-to-all-start.2) | async-done | bytes 589856 | tf_op jit(solution)/shard_map/all_to_all | solution.py:424
  100.6 0.9 merge.1
  101.5 3.3 %all-to-all-start.3 = ((bf16[4,128,128]{2,1,0:T(8,128)(2,1)}), bf16[4,128,128]{2,1,0:T(8,128)(2,1)S(1)}, u32[]{:S(2)}, u32[]{:S(2)}) async-start(bf16[4,128,128]{2,1,0:T(8,128)(2,1)} %merge.1), calls=%async_computation.3 | async-start | bytes 262144 | tf_op jit(solution)/shard_map/all_to_all | solution.py:429
  104.8 3.1 %collective-permute-start.7 = (f32[1,128]{1,0:T(1,128)S(1)}, f32[1,128]{1,0:T(1,128)S(1)}, u32[]{:S(2)}, u32[]{:S(2)}) collective-permute-start(f32[1,128]{1,0:T(1,128)S(1)} %add.19.refs_1_), channel_id=1, source_target_pairs={{2,0},{0,2},{6,4},{4,6},{3,1},{1,3},{7,5},{5,7},{10,8},{8,10},{14,... | collective-permute-start | bytes 1544 | tf_op jit(solution)/shard_map/ppermute | solution.py:387
  108.0 1.2 %collective-permute-done.7.refs_2_ = f32[1,128]{1,0:T(1,128)S(1)} collective-permute-done((f32[1,128]{1,0:T(1,128)S(1)}, f32[1,128]{1,0:T(1,128)S(1)}, u32[]{:S(2)}, u32[]{:S(2)}) %collective-permute-start.7) | collective-permute-done | bytes 544 | tf_op jit(solution)/shard_map/ppermute | solution.py:387
  109.2 0.8 norm.1
  (28 shorter events, 2.0 us)
Async XLA Ops:
  0.6 8.2 %copy-start.3 = (s32[128]{0:T(128)S(1)}, s32[128]{0:T(128)}, u32[]{:S(2)}) copy-start(s32[128]{0:T(128)} %param.13) | copy-start | bytes 1540
  2.4 22.8 %all-to-all-start = ((bf16[4,384,128]{2,1,0:T(8,128)(2,1)}), bf16[4,384,128]{2,1,0:T(8,128)(2,1)S(1)}, u32[]{:S(2)}, u32[]{:S(2)}) async-start(bf16[4,384,128]{2,1,0:T(8,128)(2,1)} %pack.1), calls=%async_computation | async-start | bytes 786432 | tf_op jit(solution)/shard_map/all_to_all | solution.py:401
  8.9 7.6 %collective-permute-start = (s32[128]{0:T(128)S(1)}, s32[128]{0:T(128)S(1)}, u32[]{:S(2)}, u32[]{:S(2)}) collective-permute-start(s32[128]{0:T(128)S(1)} %copy-done.3), channel_id=1, source_target_pairs={{0,16},{8,24},{16,32},{24,40},{32,48},{40,56},{48,64},{56,72},{64,... | collective-permute-start | bytes 1544 | tf_op jit(solution)/shard_map/ppermute | solution.py:399
  12.0 5.0 %collective-permute-start.1 = (s32[128]{0:T(128)S(1)}, s32[128]{0:T(128)S(1)}, u32[]{:S(2)}, u32[]{:S(2)}) collective-permute-start(s32[128]{0:T(128)S(1)} %copy-done.3), channel_id=1, source_target_pairs={{0,8},{8,16},{16,24},{24,32},{32,40},{40,48},{48,56},{56,64},{64,7... | collective-permute-start | bytes 1544 | tf_op jit(solution)/shard_map/ppermute | solution.py:398
  16.4 0.7 copy-start.4
  17.1 0.5 copy-start.5
  25.2 19.7 %copy-start.2 = (s32[128]{0:T(128)S(1)}, s32[128]{0:T(128)}, u32[]{:S(2)}) copy-start(s32[128]{0:T(128)} %refs_1_.5) | copy-start | bytes 1540
  26.1 18.7 %all-to-all-start.1 = ((bf16[4,4,128,128]{3,2,1,0:T(8,128)(2,1)}), bf16[4,4,128,128]{3,2,1,0:T(8,128)(2,1)S(1)}, u32[]{:S(2)}, u32[]{:S(2)}) async-start(bf16[4,4,128,128]{3,2,1,0:T(8,128)(2,1)} %broadcast_in_dim.21), calls=%async_computation.1 | async-start | bytes 1048576 | tf_op jit(solution)/shard_map/all_to_all | solution.py:413
  33.0 11.8 %collective-permute-start.3 = (bf16[4,256,128]{2,1,0:T(8,128)(2,1)S(1)}, bf16[4,256,128]{2,1,0:T(8,128)(2,1)S(1)}, u32[]{:S(2)}, u32[]{:S(2)}) collective-permute-start(bf16[4,256,128]{2,1,0:T(8,128)(2,1)S(1)} %slice.7), channel_id=1, source_target_pairs={{0,8},{8,0},{1,9},{9,1},{2,10},{10,2},{3,11},{11,3},{4,12},{12,4},... | collective-permute-start | bytes 786440 | tf_op jit(solution)/shard_map/ppermute | solution.py:414
  36.4 31.9 %collective-permute-start.2 = (bf16[4,256,128]{2,1,0:T(8,128)(2,1)S(1)}, bf16[4,256,128]{2,1,0:T(8,128)(2,1)S(1)}, u32[]{:S(2)}, u32[]{:S(2)}) collective-permute-start(bf16[4,256,128]{2,1,0:T(8,128)(2,1)S(1)} %slice.7), channel_id=1, source_target_pairs={{0,256},{256,0},{1,257},{257,1},{2,258},{258,2},{3,259},{259,3},{4... | collective-permute-start | bytes 786440 | tf_op jit(solution)/shard_map/ppermute | solution.py:411
  44.8 25.9 %copy-start.6 = (f32[1,128]{1,0:T(1,128)S(1)}, f32[1,128]{1,0:T(1,128)}, u32[]{:S(2)}) copy-start(f32[1,128]{1,0:T(1,128)} %get-tuple-element.33) | copy-start | bytes 1540
  68.3 14.4 %collective-permute-start.4 = (bf16[4,256,128]{2,1,0:T(8,128)(2,1)S(1)}, bf16[4,256,128]{2,1,0:T(8,128)(2,1)S(1)}, u32[]{:S(2)}, u32[]{:S(2)}) collective-permute-start(bf16[4,256,128]{2,1,0:T(8,128)(2,1)S(1)} %collective-permute-done.2.refs_3_), channel_id=1, source_target_pairs={{0,8},{8,0},{1,9},{9,1},{2,10},{10,2},{3,11},{11,3},{4,12},{12,4},... | collective-permute-start | bytes 786440 | tf_op jit(solution)/shard_map/ppermute | solution.py:420
  70.8 15.5 %collective-permute-start.5 = (f32[1,128]{1,0:T(1,128)S(1)}, f32[1,128]{1,0:T(1,128)S(1)}, u32[]{:S(2)}, u32[]{:S(2)}) collective-permute-start(f32[1,128]{1,0:T(1,128)S(1)} %copy-done.6), channel_id=1, source_target_pairs={{0,1},{1,0},{2,3},{3,2},{4,5},{5,4},{6,7},{7,6},{8,9},{9,8},{10,11... | collective-permute-start | bytes 1544 | tf_op jit(solution)/shard_map/ppermute | solution.py:416
  86.2 22.9 %copy-start = (f32[128,1024]{1,0:T(8,128)S(1)}, f32[128,1024]{1,0:T(8,128)}, u32[]{:S(2)}) copy-start(f32[128,1024]{1,0:T(8,128)} %get-tuple-element.36.refs_0_) | copy-start | bytes 1572868
  86.2 22.9 %copy-start.1 = (f32[1024]{0:T(1024)S(1)}, f32[1024]{0:T(1024)}, u32[]{:S(2)}) copy-start(f32[1024]{0:T(1024)} %param.17) | copy-start | bytes 12292
  86.3 14.4 %all-to-all-start.2 = ((bf16[4,144,512]{2,1,0:T(8,128)(2,1)}), bf16[4,144,512]{2,1,0:T(8,128)(2,1)S(1)}, u32[]{:S(2)}, u32[]{:S(2)}) async-start(bf16[4,144,512]{2,1,0:T(8,128)(2,1)} %attend_last.1), calls=%async_computation.2 | async-start | bytes 1179648 | tf_op jit(solution)/shard_map/all_to_all | solution.py:424
  90.9 5.8 %collective-permute-start.6 = (f32[1,128]{1,0:T(1,128)S(1)}, f32[1,128]{1,0:T(1,128)S(1)}, u32[]{:S(2)}, u32[]{:S(2)}) collective-permute-start(f32[1,128]{1,0:T(1,128)S(1)} %add.18), channel_id=1, source_target_pairs={{4,0},{6,2},{0,4},{2,6},{5,1},{7,3},{1,5},{3,7},{12,8},{14,10},{8,... | collective-permute-start | bytes 1544 | tf_op jit(solution)/shard_map/ppermute | solution.py:387
  101.5 8.5 %all-to-all-start.3 = ((bf16[4,128,128]{2,1,0:T(8,128)(2,1)}), bf16[4,128,128]{2,1,0:T(8,128)(2,1)S(1)}, u32[]{:S(2)}, u32[]{:S(2)}) async-start(bf16[4,128,128]{2,1,0:T(8,128)(2,1)} %merge.1), calls=%async_computation.3 | async-start | bytes 262144 | tf_op jit(solution)/shard_map/all_to_all | solution.py:429
  104.8 4.3 %collective-permute-start.7 = (f32[1,128]{1,0:T(1,128)S(1)}, f32[1,128]{1,0:T(1,128)S(1)}, u32[]{:S(2)}, u32[]{:S(2)}) collective-permute-start(f32[1,128]{1,0:T(1,128)S(1)} %add.19.refs_1_), channel_id=1, source_target_pairs={{2,0},{0,2},{6,4},{4,6},{3,1},{1,3},{7,5},{5,7},{10,8},{8,10},{14,... | collective-permute-start | bytes 1544 | tf_op jit(solution)/shard_map/ppermute | solution.py:387
